TPU v7x, 32 devices: a whole 2x2x4 slice. The times are simulated.
32 devices in a mesh: band: 4 (over x, core), slab: 8 (over z, y).
Axes of the slice: x: 2, y: 2, z: 4, core: 2. Of those that a mesh axis runs over, the one named last changes fastest.
Arguments:
- orbitals: float32 [16, 128, 128, 128], P('band', 'slab'), may hold values from -6 to 6
- occupations: float32 [16], P('band'), may hold values from 0.1 to 1
- accumulated: float32 [16, 128, 128, 128], P('band', 'slab'), may hold values from -6 to 6
Outputs:
- exchange_terms: float32 [16, 128, 128, 128], P('band', 'slab')
All inputs are finite; a program needn't handle non-finite values.
Results may differ from a plain program's by a relative error of at most 0.00012.
Values sent between devices are 32-bit elements; how exact they have to be, the bound alone decides.
No kernel may reach another device: no remote copies, remote signals or barrier semaphores. Data moves between devices by JAX's collectives and lax.ppermute only.
A program may use at most 128 MiB of HBM per device.

v0:
```python
import math

import jax
import jax.numpy as jnp
from jax import lax
from jax.experimental import pallas as pl
from jax.experimental.pallas import tpu as pltpu
from jax.sharding import PartitionSpec as P


HOPS = 3
CORES = 2
AXES = ("band", "slab")


def shifted(value, axis, steps):
    count = lax.axis_size(axis)
    pairs = [(source, (source + steps) % count) for source in range(count)]
    return lax.ppermute(value, axis, pairs)


def hartley_rows(rows, extent):
    index = jnp.arange(extent, dtype=jnp.int32)
    product = rows[:, None] * index[None, :] % extent
    angle = product.astype(jnp.float32) * (2.0 * math.pi / extent)
    return jnp.cos(angle) + jnp.sin(angle)


def hartley_matrix(extent):
    return hartley_rows(jnp.arange(extent, dtype=jnp.int32), extent)


def signed_wave(index, extent):
    signed = jnp.where(index < extent // 2, index, index - extent)
    return signed.astype(jnp.float32) * (2.0 * math.pi / extent)


def slab_body(orbitals, occupations, accumulated):
    extent = orbitals.shape[2]
    planes = orbitals.shape[1]
    matrix = hartley_matrix(extent)
    full_index = jnp.arange(extent, dtype=jnp.int32)
    local_index = lax.axis_index("slab") * planes + jnp.arange(planes, dtype=jnp.int32)
    wave_full = signed_wave(full_index, extent)
    wave_local = signed_wave(local_index, extent)
    square = (
        wave_full[:, None, None] ** 2
        + wave_local[None, :, None] ** 2
        + wave_full[None, None, :] ** 2
    )
    screening = 4.0 * math.pi / (square + 0.01) / float(extent**3)
    highest = lax.Precision.HIGHEST

    def transform_inner(values):
        spectra = jnp.einsum("pxyz,zc->pxyc", values, matrix, precision=highest)
        return jnp.einsum("pxyc,yb->pxbc", spectra, matrix, precision=highest)

    leading = orbitals[0]
    leading_occ = occupations[0:1]
    carried = (leading, leading_occ)
    visits = []
    for _ in range(HOPS):
        carried = shifted((carried[0], carried[1]), "band", 1)
        visits.append(carried)
    result = accumulated
    for visitor, visitor_occ in visits:
        potentials_spectra = transform_inner(orbitals * visitor[None])
        columns = jnp.einsum(
            "pxbc,xa->pabc",
            lax.all_to_all(potentials_spectra, "slab", split_axis=2, concat_axis=1, tiled=True),
            matrix,
            precision=highest,
        )
        columns = columns * screening[None]
        columns = jnp.einsum("pabc,ax->pxbc", columns, matrix, precision=highest)
        returned = lax.all_to_all(columns, "slab", split_axis=1, concat_axis=2, tiled=True)
        potential = transform_inner(returned)
        result = result - visitor_occ[0] * visitor[None] * potential
    return result


def halves(values):
    head = values.astype(jnp.bfloat16)
    return head, (values - head.astype(jnp.float32)).astype(jnp.bfloat16)


def rounded_halves(matrix):
    head = lax.reduce_precision(matrix, exponent_bits=8, mantissa_bits=7)
    return head.astype(jnp.bfloat16), (matrix - head).astype(jnp.bfloat16)


def right_factor(matrix):
    head, tail = rounded_halves(matrix)
    return jnp.concatenate(
        [
            jnp.concatenate([head, tail], 1),
            jnp.concatenate([head, jnp.zeros_like(tail)], 1),
        ],
        0,
    )


def left_factor(matrix):
    head, tail = rounded_halves(matrix)
    return jnp.concatenate(
        [
            jnp.concatenate([head, head], 1),
            jnp.concatenate([tail, jnp.zeros_like(tail)], 1),
        ],
        0,
    )


def times_right(rows, factor):
    width = rows.shape[1]
    out = jnp.dot(
        jnp.concatenate(halves(rows), 1), factor, preferred_element_type=jnp.float32
    )
    return out[:, :width] + out[:, width:]


def times_left(factor, columns):
    out = jnp.dot(
        factor, jnp.concatenate(halves(columns), 0), preferred_element_type=jnp.float32
    )
    height = out.shape[0] // 2
    return out[:height] + out[height:]


def forward_kernel(flag_ref, own_ref, beside_ref, *refs):
    residents = refs[:4]
    right_ref, left_ref, kept_ref, sent_ref = refs[4:]
    keep = kept_ref.shape[0]
    places, depth, _, width = own_ref.shape
    flip = flag_ref[0] == 1
    for place in range(places):
        first, second = residents[2 * place], residents[2 * place + 1]
        for e in range(2):
            visitor = (own_ref, beside_ref)[e]
            made = []
            for plane in range(0, depth, 2):
                pair = []
                for p in (plane, plane + 1):
                    if e == 0:
                        resident = jnp.where(flip, second[p], first[p])
                    else:
                        resident = jnp.where(flip, first[p], second[p])
                    pair.append(times_right(resident * visitor[place, p], right_ref[...]))
                both = times_left(left_ref[...], jnp.concatenate(pair, 1))
                made.append(both[:, :width])
                made.append(both[:, width:])
            block = jnp.transpose(jnp.stack(made, 0), (1, 0, 2))
            at = (2 * place + e) * depth
            kept_ref[:, at : at + depth, :] = block[:keep]
            sent_ref[:, at : at + depth, :] = block[keep:]


def across_kernel(a_ref, b_ref, c_ref, d_ref, screen_ref, forth_ref, back_ref, *outs):
    parts = (a_ref, b_ref, c_ref, d_ref)
    count, depth, width = a_ref.shape
    for row in range(0, count, 2):
        columns = jnp.concatenate(
            [
                jnp.concatenate([part[row], part[row + 1]], 1)
                for part in parts
            ],
            0,
        )
        spectrum = times_left(forth_ref[...], columns)
        spectrum = spectrum * jnp.concatenate([screen_ref[row], screen_ref[row + 1]], 1)
        lines = times_left(back_ref[...], spectrum)
        for index, out in enumerate(outs):
            out[row] = lines[index * depth : (index + 1) * depth, :width]
            out[row + 1] = lines[index * depth : (index + 1) * depth, width:]


def inverse_kernel(flag_ref, weight_ref, right_ref, left_ref, *refs):
    outs = refs[-4:]
    groups = [refs[4 * index : 4 * index + 4] for index in range(len(refs) // 4 - 1)]
    places, depth, extent, width = groups[0][2].shape
    flip = flag_ref[0] == 1

    def potentials(own_ref, other_ref, slot):
        at = slice(slot * depth, (slot + 1) * depth)
        rows = jnp.concatenate([own_ref[:, at, :], other_ref[:, at, :]], 0)
        rows = times_right(rows.reshape(extent * depth, width), right_ref[...])
        block = jnp.transpose(rows.reshape(extent, depth, width), (1, 0, 2))
        made = []
        for plane in range(0, depth, 2):
            both = times_left(
                left_ref[...], jnp.concatenate([block[plane], block[plane + 1]], 1)
            )
            made += [both[:, :width], both[:, width:]]
        return made

    for place in range(places):
        sums = [[None] * depth, [None] * depth]
        for e in range(2):
            for index, (own_ref, other_ref, near_ref, beside_ref) in enumerate(groups):
                made = potentials(own_ref, other_ref, 2 * place + e)
                visitor = (near_ref, beside_ref)[e]
                for p in range(depth):
                    term = weight_ref[index] * visitor[place, p] * made[p]
                    sums[e][p] = term if index == 0 else sums[e][p] + term
        for p in range(depth):
            outs[2 * place][p] = jnp.where(flip, sums[1][p], sums[0][p])
            outs[2 * place + 1][p] = jnp.where(flip, sums[0][p], sums[1][p])


def vmem(count):
    return [pl.BlockSpec(memory_space=pltpu.VMEM)] * count


def smem(count):
    return [pl.BlockSpec(memory_space=pltpu.SMEM)] * count


def chip_body(orbitals, occupations, accumulated):
    _, planes, extent, width = orbitals.shape
    bands, slabs = lax.axis_size("band"), lax.axis_size("slab")
    lines = slabs // 2
    depth = planes // CORES
    band, slab = lax.axis_index("band"), lax.axis_index("slab")
    core, side = band % CORES, slab % 2
    line = slab // 2

    def moved(value, to):
        pairs = []
        for x in range(bands // CORES):
            for c in range(CORES):
                for z in range(lines):
                    for y in range(2):
                        target = to(x, c, z, y)
                        if target is not None:
                            tx, tc, tz, ty = target
                            pairs.append(
                                (
                                    (x * CORES + c) * slabs + z * 2 + y,
                                    (tx * CORES + tc) * slabs + tz * 2 + ty,
                                )
                            )
        return lax.ppermute(value, AXES, pairs)

    over_core = lambda x, c, z, y: (x, c ^ 1, z, y)
    over_x = lambda x, c, z, y: (x ^ 1, c, z, y)
    over_y = lambda x, c, z, y: (x, c, z, y ^ 1)
    over_z = lambda x, c, z, y: (x, c, z ^ 1, y)
    over_middle = lambda x, c, z, y: (x, c, z ^ 3, y) if z in (1, 2) else None
    outward = lambda x, c, z, y: (x, c, z ^ 1, y) if z in (1, 2) else None

    def piece(orbital, half, source=None):
        return lax.dynamic_slice(
            orbitals if source is None else source, (orbital, half * depth, 0, 0), (1, depth, extent, width)
        )[0]

    zero = jnp.int32(0)
    kept_half = piece(zero, core)
    swapped_half = moved(piece(zero, 1 - core), over_core)
    same = core == side
    leads = jnp.stack(
        [jnp.where(same, kept_half, swapped_half), jnp.where(same, swapped_half, kept_half)]
    )

    def shares(bits):
        return moved(occupations[0:1], lambda x, c, z, y: (x ^ (bits // 2), c ^ (bits % 2), z, y))

    all_shares = jnp.concatenate([occupations[0:1]] + [shares(bits) for bits in range(1, bands)])

    def share(x_bit, owner):
        return lax.dynamic_slice(all_shares, (x_bit * 2 + (core ^ owner),), (1,))

    held = [[None, None] for _ in range(lines)]

    def fetch(m, t):
        held[m][t] = moved(
            piece(line ^ m, core ^ side ^ t), lambda x, c, z, y: (x, c ^ y ^ t, z ^ m, c)
        )

    weights = jnp.concatenate([share(0, 1 - side), share(1, side), share(1, 1 - side)])
    orbitals, leads = lax.optimization_barrier((orbitals, leads))
    for m in range(lines):
        for t in range(2):
            fetch(m, t)

    leads_z = moved(leads, over_z)
    far_x = [moved(leads, over_x), moved(leads_z, over_x)]
    leads_z, weights = lax.optimization_barrier((leads_z, weights))
    near = [jnp.stack([leads[row], leads_z[row]]) for row in range(2)]
    inner = [moved(near[row], over_middle) for row in range(2)]
    beside_near = moved(near[0], over_y)
    middle = (line == 1) | (line == 2)
    outer = [moved(inner[row], outward) for row in range(2)]
    far = [jnp.where(middle, inner[row][::-1], outer[row]) for row in range(2)]
    x_near = [jnp.stack([far_x[0][row], far_x[1][row]]) for row in range(2)]
    x_beside_near = moved(beside_near, over_x)
    x_far = [moved(far[row], over_x) for row in range(2)]
    beside_far = moved(far[0], over_y)
    x_mine_beside_near = moved(x_near[1], over_y)
    x_beside_far = moved(beside_far, over_x)
    x_mine_beside_far = moved(x_far[1], over_y)
    visitors = [
        ((near[1], beside_near), (far[1], beside_far)),
        ((x_near[0], x_mine_beside_near), (x_far[0], x_mine_beside_far)),
        ((x_near[1], x_beside_near), (x_far[1], x_beside_far)),
    ]


    natural = jnp.arange(extent, dtype=jnp.int32)
    matrix = hartley_matrix(extent)
    keep = extent // CORES
    order_b = (natural + core * keep) % extent
    steps = jnp.arange(lines, dtype=jnp.int32)
    sides = jnp.arange(2, dtype=jnp.int32)
    offsets = jnp.arange(depth, dtype=jnp.int32)
    spots = (
        (line ^ steps)[:, None, None] * (2 * planes)
        + (side ^ sides)[None, :, None] * planes
        + offsets[None, None, :]
    ).reshape(-1)
    order_x = jnp.concatenate([spots + core * depth, spots + (1 - core) * depth])
    rows_b = hartley_rows(order_b, extent)
    rows_x = hartley_rows(order_x, extent)
    right = right_factor(matrix)
    left_b_forth = left_factor(rows_b)
    left_b_back = left_factor(rows_b.T)
    left_x_forth = left_factor(rows_x.T)
    left_x_back = left_factor(rows_x)
    wave = signed_wave(natural, extent)
    wave_b = signed_wave(order_b[:keep], extent)
    square = wave_b[:, None, None] ** 2 + wave[None, :, None] ** 2 + wave[None, None, :] ** 2
    screen = 4.0 * math.pi / (square + 0.01) / float(extent**3)

    flag = core.reshape(1).astype(jnp.int32)
    group = lines // 2 * 2 * depth
    spectrum_shape = jax.ShapeDtypeStruct((keep, group, width), jnp.float32)
    piece_shape = jax.ShapeDtypeStruct((depth, extent, width), jnp.float32)
    params = pltpu.CompilerParams(vmem_limit_bytes=24 * 1024 * 1024)

    def forward(index, part):
        pieces = [held[m][t] for m in (2 * part, 2 * part + 1) for t in range(2)]
        return pl.pallas_call(
            forward_kernel,
            out_shape=(spectrum_shape, spectrum_shape),
            in_specs=smem(1) + vmem(8),
            out_specs=tuple(vmem(2)),
            compiler_params=params,
            name="forward",
        )(flag, *visitors[index][part], *pieces, right, left_b_forth)

    def across(parts):
        return pl.pallas_call(
            across_kernel,
            out_shape=(spectrum_shape,) * 4,
            in_specs=vmem(7),
            out_specs=tuple(vmem(4)),
            compiler_params=params,
            name="across",
        )(*parts, screen, left_x_forth, left_x_back)

    def inverse(part, spectra):
        operands = []
        for index, pair in enumerate(spectra):
            operands += [*pair, *visitors[index][part]]
        return pl.pallas_call(
            inverse_kernel,
            out_shape=(piece_shape,) * 4,
            in_specs=smem(2) + vmem(len(operands) + 2),
            out_specs=tuple(vmem(4)),
            compiler_params=params,
            name="inverse",
        )(flag, weights, right, left_b_back, *operands)

    spectra = [[], []]
    for index in range(HOPS):
        kept, got = [], []
        for part in range(2):
            own, sent = forward(index, part)
            kept.append(own)
            got.append(moved(sent, over_core))
        out = across(kept + got)
        for part in range(2):
            spectra[part].append((out[part], moved(out[2 + part], over_core)))

    result = accumulated
    for part in (1, 0):
        terms = inverse(part, spectra[part])
        for place in range(2):
            for t in range(2):
                m = 2 * part + place
                back = moved(
                    terms[2 * place + t],
                    lambda x, c, z, y: (x, y, z ^ m, c ^ y ^ t),
                )
                start = (line ^ m, (core ^ side ^ t) * depth, 0, 0)
                old = lax.dynamic_slice(accumulated, start, (1, depth, extent, width))
                result = lax.dynamic_update_slice(result, old - back[None], start)
    return result


def solution(mesh):
    bands, slabs = mesh.shape["band"], mesh.shape["slab"]

    def body(orbitals, occupations, accumulated):
        residents, planes = orbitals.shape[:2]
        one_each = bands == HOPS + 1 and slabs == 2 * residents and residents == 2 * CORES
        if one_each and planes % (8 * CORES) == 0:
            return chip_body(orbitals, occupations, accumulated)
        return slab_body(orbitals, occupations, accumulated)

    in_specs = (P("band", "slab", None, None), P("band"), P("band", "slab", None, None))
    out_specs = P("band", "slab", None, None)
    return jax.shard_map(
        body, mesh=mesh, in_specs=in_specs, out_specs=out_specs, check_vma=False
    )
```

profile of v0, /device:TPU:0, one launch (start us, length us, event | category | flops | bytes accessed | tf_op | source)
XLA Modules:
  0.0 392.5 jit_solution(1236041726947771895)
XLA Ops:
  0.0 1.1 dynamic-slice_bitcast_fusion.8
  1.7 1.5 collective-permute-done
  3.2 1.1 fusion.8
  4.4 3.0 collective-permute-start.1
  7.4 1.5 collective-permute-start.3
  9.3 1.8 collective-permute-done.3
  11.1 0.9 collective-permute-done.4
  12.0 1.9 pad_maximum_fusion.5
  14.6 2.0 pad_maximum_fusion.6.weight_ref
  16.6 14.3 %collective-permute-done.1 = f32[2,8,128,128]{3,2,1,0:T(8,128)} collective-permute-done((f32[2,8,128,128]{3,2,1,0:T(8,128)S(1)}, f32[2,8,128,128]{3,2,1,0:T(8,128)}, u32[]{:S(2)}, u32[]{:S(2)}) %collective-permute-start.1) | collective-permute-done | bytes 1048608 | tf_op jit(solution)/shard_map/ppermute | solution.py:242
  31.0 1.3 fusion.67
  32.3 1.0 pad_maximum_fusion.2
  33.3 1.6 collective-permute-start.12
  35.0 1.7 collective-permute-start.10
  36.7 4.0 %dynamic-slice_bitcast_fusion = (f32[8,128,128]{2,1,0:T(8,128)S(1)}, f32[8,128,128]{2,1,0:T(8,128)}, f32[8,128,128]{2,1,0:T(8,128)}, f32[8,128,128]{2,1,0:T(8,12...) fusion(f32[4,16,128,128]{3,2,1,0:T(8,128)} %param.3, ...), kind=kLoop, calls=%fused_computation.28 | loop fusion | bytes 8388632 | tf_op jit(solution)/shard_map/squeeze | solution.py:252
  40.7 5.4 %collective-permute-start.15 = (f32[8,128,128]{2,1,0:T(8,128)}, f32[8,128,128]{2,1,0:T(8,128)S(1)}, u32[]{:S(2)}, u32[]{:S(2)}) collective-permute-start(f32[8,128,128]{2,1,0:T(8,128)} %get-tuple-element.82), channel_id=1, source_target_pairs={{0,4},{1,12},{2,6},{3,14},{4,0},{5,8},{6,2},{7,10},{8,13},{9,5},{1... | collective-permute-start | bytes 1572872 | tf_op jit(solution)/shard_map/ppermute | solution.py:242
  46.1 1.3 collective-permute-start.17
  47.5 1.3 collective-permute-start.13
  48.8 1.3 collective-permute-start.11
  50.1 80.0 %collective-permute-done.15.refs_0_ = f32[8,128,128]{2,1,0:T(8,128)S(1)} collective-permute-done((f32[8,128,128]{2,1,0:T(8,128)}, f32[8,128,128]{2,1,0:T(8,128)S(1)}, u32[]{:S(2)}, u32[]{:S(2)}) %collective-permute-start.15) | collective-permute-done | bytes 524320 | tf_op jit(solution)/shard_map/ppermute | solution.py:242
  130.1 1.5 collective-permute-start.22
  131.6 10.6 %collective-permute-done.16.refs_1_ = f32[8,128,128]{2,1,0:T(8,128)S(1)} collective-permute-done((f32[8,128,128]{2,1,0:T(8,128)}, f32[8,128,128]{2,1,0:T(8,128)S(1)}, u32[]{:S(2)}, u32[]{:S(2)}) %collective-permute-start.16) | collective-permute-done | bytes 524320 | tf_op jit(solution)/shard_map/ppermute | solution.py:242
  142.3 1.5 collective-permute-start.23
  144.4 1.7 collective-permute-start.6
  146.1 17.5 %collective-permute-done.11 = f32[2,8,128,128]{3,2,1,0:T(8,128)} collective-permute-done((f32[2,8,128,128]{3,2,1,0:T(8,128)}, f32[2,8,128,128]{3,2,1,0:T(8,128)}, u32[]{:S(2)}, u32[]{:S(2)}) %collective-permute-start.11) | collective-permute-done | bytes 1048608 | tf_op jit(solution)/shard_map/ppermute | solution.py:242
  163.6 1.9 collective-permute-start.7
  165.5 1.7 reverse_select_fusion
  167.2 1.7 reverse_select_fusion.1.own_ref.refs_2_
  169.0 10.3 %collective-permute-done.7.refs_1_ = f32[8,128,128]{2,1,0:T(8,128)S(1)} collective-permute-done((f32[8,128,128]{2,1,0:T(8,128)}, f32[8,128,128]{2,1,0:T(8,128)S(1)}, u32[]{:S(2)}, u32[]{:S(2)}) %collective-permute-start.7) | collective-permute-done | bytes 524320 | tf_op jit(solution)/shard_map/ppermute | solution.py:242
  179.3 4.1 %collective-permute-start.9 = (f32[8,128,128]{2,1,0:T(8,128)S(1)}, f32[8,128,128]{2,1,0:T(8,128)S(1)}, u32[]{:S(2)}, u32[]{:S(2)}) collective-permute-start(f32[8,128,128]{2,1,0:T(8,128)S(1)} %copy-done.4), channel_id=1, source_target_pairs={{0,10},{1,2},{2,8},{3,0},{4,14},{5,6},{6,12},{7,4},{8,3},{9,11},{1... | collective-permute-start | bytes 1572872 | tf_op jit(solution)/shard_map/ppermute | solution.py:242
  183.3 1.5 collective-permute-start.31
  185.4 1.3 fusion.64
  186.7 1.3 fusion.65
  188.2 2.6 collective-permute-start.18
  190.8 8.7 %collective-permute-done.9.refs_3_ = f32[8,128,128]{2,1,0:T(8,128)S(1)} collective-permute-done((f32[8,128,128]{2,1,0:T(8,128)S(1)}, f32[8,128,128]{2,1,0:T(8,128)S(1)}, u32[]{:S(2)}, u32[]{:S(2)}) %collective-permute-start.9) | collective-permute-done | bytes 524320 | tf_op jit(solution)/shard_map/ppermute | solution.py:242
  200.2 3.1 forward.6
  203.3 6.4 %collective-permute-done.18.refs_3_ = f32[8,128,128]{2,1,0:T(8,128)S(1)} collective-permute-done((f32[8,128,128]{2,1,0:T(8,128)S(1)}, f32[8,128,128]{2,1,0:T(8,128)S(1)}, u32[]{:S(2)}, u32[]{:S(2)}) %collective-permute-start.18) | collective-permute-done | bytes 524320 | tf_op jit(solution)/shard_map/ppermute | solution.py:242
  209.6 1.5 collective-permute-start.25
  211.1 10.2 %collective-permute-done.14.beside_ref.refs_3_ = f32[2,8,128,128]{3,2,1,0:T(8,128)S(1)} collective-permute-done((f32[2,8,128,128]{3,2,1,0:T(8,128)S(1)}, f32[2,8,128,128]{3,2,1,0:T(8,128)S(1)}, u32[]{:S(2)}, u32[]{:S(2)}) %collective-permute-start.14) | collective-permute-done | bytes 1048608 | tf_op jit(solution)/shard_map/ppermute | solution.py:242
  221.3 1.0 collective-permute-start.32
  222.4 8.5 %collective-permute-done.26.own_ref.refs_10_ = f32[2,8,128,128]{3,2,1,0:T(8,128)S(1)} collective-permute-done((f32[2,8,128,128]{3,2,1,0:T(8,128)S(1)}, f32[2,8,128,128]{3,2,1,0:T(8,128)S(1)}, u32[]{:S(2)}, u32[]{:S(2)}) %collective-permute-start.26) | collective-permute-done | bytes 1048608 | tf_op jit(solution)/shard_map/ppermute | solution.py:242
  232.1 1.8 forward.7
  233.9 9.9 %collective-permute-done.24.beside_ref.refs_7_ = f32[2,8,128,128]{3,2,1,0:T(8,128)S(1)} collective-permute-done((f32[2,8,128,128]{3,2,1,0:T(8,128)S(1)}, f32[2,8,128,128]{3,2,1,0:T(8,128)S(1)}, u32[]{:S(2)}, u32[]{:S(2)}) %collective-permute-start.24) | collective-permute-done | bytes 1048608 | tf_op jit(solution)/shard_map/ppermute | solution.py:242
  243.8 1.1 collective-permute-start.20
  245.1 1.8 forward.10
  246.9 1.8 forward.8
  248.8 27.0 %collective-permute-done.32.beside_ref.refs_11_ = f32[2,8,128,128]{3,2,1,0:T(8,128)S(1)} collective-permute-done((f32[2,8,128,128]{3,2,1,0:T(8,128)S(1)}, f32[2,8,128,128]{3,2,1,0:T(8,128)S(1)}, u32[]{:S(2)}, u32[]{:S(2)}) %collective-permute-start.32) | collective-permute-done | bytes 1048608 | tf_op jit(solution)/shard_map/ppermute | solution.py:242
  275.8 1.1 collective-permute-start.33
  276.8 1.8 forward.11
  279.2 2.8 forward.9
  282.1 1.4 divide_multiply_fusion.screen_ref
  283.5 2.5 across.3
  286.5 2.5 across.5
  289.2 2.5 across.4
  292.9 1.7 collective-permute-done.30.refs_5_
  294.5 5.2 %inverse.2 = (f32[8,128,128]{2,1,0:T(8,128)S(1)}, f32[8,128,128]{2,1,0:T(8,128)S(1)}, f32[8,128,128]{2,1,0:T(8,128)S(1)}, f32[8,128,128]{2,1,0:T(8,128)S(1)}) custom-call(s32[1]{0:T(128)} %bitcast.flag_ref, f32[3]{0:T(128)S(1)} %pad_maximum_fusion.6.weight_ref, bf16[256,256]{1,0:T(8,128)(2,1)S(1)} %fusion.15.refs_4_.right_ref, ...), custom_call_target="tpu_custom_call" | custom-call | tf_op jit(solution)/shard_map/inverse/pallas_call | solution.py:364
  300.2 5.8 %inverse.3 = (f32[8,128,128]{2,1,0:T(8,128)S(1)}, f32[8,128,128]{2,1,0:T(8,128)S(1)}, f32[8,128,128]{2,1,0:T(8,128)S(1)}, f32[8,128,128]{2,1,0:T(8,128)S(1)}) custom-call(s32[1]{0:T(128)} %bitcast.flag_ref, f32[3]{0:T(128)S(1)} %pad_maximum_fusion.6.weight_ref, bf16[256,256]{1,0:T(8,128)(2,1)S(1)} %fusion.15.refs_4_.right_ref, ...), custom_call_target="tpu_custom_call" | custom-call | tf_op jit(solution)/shard_map/inverse/pallas_call | solution.py:364
  306.7 8.4 %collective-permute-start.39 = (f32[8,128,128]{2,1,0:T(8,128)S(1)}, f32[8,128,128]{2,1,0:T(8,128)S(1)}, u32[]{:S(2)}, u32[]{:S(2)}) collective-permute-start(f32[8,128,128]{2,1,0:T(8,128)S(1)} %get-tuple-element.66), channel_id=1, source_target_pairs={{0,7},{1,14},{2,5},{3,12},{4,3},{5,10},{6,1},{7,8},{8,6},{9,15},{1... | collective-permute-start | bytes 1572872 | tf_op jit(solution)/shard_map/ppermute | solution.py:242
  315.1 40.7 %collective-permute-done.36 = f32[8,128,128]{2,1,0:T(8,128)S(1)} collective-permute-done((f32[8,128,128]{2,1,0:T(8,128)S(1)}, f32[8,128,128]{2,1,0:T(8,128)S(1)}, u32[]{:S(2)}, u32[]{:S(2)}) %collective-permute-start.36) | collective-permute-done | bytes 524320 | tf_op jit(solution)/shard_map/ppermute | solution.py:242
  355.7 2.0 collective-permute-start.44
  357.9 7.7 %collective-permute-done.37 = f32[8,128,128]{2,1,0:T(8,128)S(1)} collective-permute-done((f32[8,128,128]{2,1,0:T(8,128)S(1)}, f32[8,128,128]{2,1,0:T(8,128)S(1)}, u32[]{:S(2)}, u32[]{:S(2)}) %collective-permute-start.37) | collective-permute-done | bytes 524320 | tf_op jit(solution)/shard_map/ppermute | solution.py:242
  365.6 1.7 collective-permute-start.45
  367.4 10.9 %collective-permute-start.46 = (f32[8,128,128]{2,1,0:T(8,128)S(1)}, f32[8,128,128]{2,1,0:T(8,128)S(1)}, u32[]{:S(2)}, u32[]{:S(2)}) collective-permute-start(f32[8,128,128]{2,1,0:T(8,128)S(1)} %get-tuple-element.76), channel_id=1, source_target_pairs={{0,3},{1,10},{2,1},{3,8},{4,7},{5,14},{6,5},{7,12},{8,2},{9,11},{1... | collective-permute-start | bytes 1572872 | tf_op jit(solution)/shard_map/ppermute | solution.py:242
  378.8 12.8 %collective-permute-done.46 = f32[8,128,128]{2,1,0:T(8,128)S(1)} collective-permute-done((f32[8,128,128]{2,1,0:T(8,128)S(1)}, f32[8,128,128]{2,1,0:T(8,128)S(1)}, u32[]{:S(2)}, u32[]{:S(2)}) %collective-permute-start.46) | collective-permute-done | bytes 524320 | tf_op jit(solution)/shard_map/ppermute | solution.py:242
  (99 shorter events, 10.4 us)
Async XLA Ops:
  0.0 7.4 %copy-start.6 = (f32[4]{0:T(128)S(1)}, f32[4]{0:T(128)}, u32[]{:S(2)}) copy-start(f32[4]{0:T(128)} %param.4) | copy-start | bytes 52
  1.1 2.1 collective-permute-start
  4.4 30.5 %copy-start.3 = (f32[2,8,128,128]{3,2,1,0:T(8,128)}, f32[2,8,128,128]{3,2,1,0:T(8,128)S(1)}, u32[]{:S(2)}) copy-start(f32[2,8,128,128]{3,2,1,0:T(8,128)S(1)} %pad_maximum_fusion) | copy-start | bytes 3145732
  4.4 26.6 %collective-permute-start.1 = (f32[2,8,128,128]{3,2,1,0:T(8,128)S(1)}, f32[2,8,128,128]{3,2,1,0:T(8,128)}, u32[]{:S(2)}, u32[]{:S(2)}) collective-permute-start(f32[2,8,128,128]{3,2,1,0:T(8,128)S(1)} %pad_maximum_fusion), channel_id=1, source_target_pairs={{0,2},{1,3},{2,0},{3,1},{4,6},{5,7},{6,4},{7,5},{8,10},{9,11},{10,... | collective-permute-start | bytes 3145736 | tf_op jit(solution)/shard_map/ppermute | solution.py:242
  7.4 1.9 collective-permute-start.2
  7.4 3.7 collective-permute-start.3
  8.9 3.1 collective-permute-start.4
  33.3 14.2 %collective-permute-start.12 = (f32[2,8,128,128]{3,2,1,0:T(8,128)}, f32[2,8,128,128]{3,2,1,0:T(8,128)}, u32[]{:S(2)}, u32[]{:S(2)}) collective-permute-start(f32[2,8,128,128]{3,2,1,0:T(8,128)} %pad_maximum_fusion.2), channel_id=1, source_target_pairs={{2,4},{3,5},{4,2},{5,3},{10,12},{11,13},{12,10},{13,11},{18,20},{1... | collective-permute-start | bytes 3145736 | tf_op jit(solution)/shard_map/ppermute | solution.py:242
  35.0 13.7 %collective-permute-start.10 = (f32[2,8,128,128]{3,2,1,0:T(8,128)S(1)}, f32[2,8,128,128]{3,2,1,0:T(8,128)}, u32[]{:S(2)}, u32[]{:S(2)}) collective-permute-start(f32[2,8,128,128]{3,2,1,0:T(8,128)S(1)} %pad_maximum_fusion.1.own_ref.refs_2_), channel_id=1, source_target_pairs={{2,4},{3,5},{4,2},{5,3},{10,12},{11,13},{12,10},{13,11},{18,20},{1... | collective-permute-start | bytes 3145736 | tf_op jit(solution)/shard_map/ppermute | solution.py:242
  40.7 89.4 %collective-permute-start.15 = (f32[8,128,128]{2,1,0:T(8,128)}, f32[8,128,128]{2,1,0:T(8,128)S(1)}, u32[]{:S(2)}, u32[]{:S(2)}) collective-permute-start(f32[8,128,128]{2,1,0:T(8,128)} %get-tuple-element.82), channel_id=1, source_target_pairs={{0,4},{1,12},{2,6},{3,14},{4,0},{5,8},{6,2},{7,10},{8,13},{9,5},{1... | collective-permute-start | bytes 1572872 | tf_op jit(solution)/shard_map/ppermute | solution.py:242
  46.1 96.1 %collective-permute-start.16 = (f32[8,128,128]{2,1,0:T(8,128)}, f32[8,128,128]{2,1,0:T(8,128)S(1)}, u32[]{:S(2)}, u32[]{:S(2)}) collective-permute-start(f32[8,128,128]{2,1,0:T(8,128)} %get-tuple-element.81), channel_id=1, source_target_pairs={{0,12},{1,4},{2,14},{3,6},{4,8},{5,0},{6,10},{7,2},{8,5},{9,13},{1... | collective-permute-start | bytes 1572872 | tf_op jit(solution)/shard_map/ppermute | solution.py:242
  46.1 96.1 %collective-permute-start.17 = (f32[8,128,128]{2,1,0:T(8,128)}, f32[8,128,128]{2,1,0:T(8,128)S(1)}, u32[]{:S(2)}, u32[]{:S(2)}) collective-permute-start(f32[8,128,128]{2,1,0:T(8,128)} %get-tuple-element.80), channel_id=1, source_target_pairs={{0,6},{1,14},{2,4},{3,12},{4,2},{5,10},{6,0},{7,8},{8,15},{9,7},{1... | collective-permute-start | bytes 1572872 | tf_op jit(solution)/shard_map/ppermute | solution.py:242
  47.5 96.9 %collective-permute-start.13 = (f32[2,8,128,128]{3,2,1,0:T(8,128)}, f32[2,8,128,128]{3,2,1,0:T(8,128)}, u32[]{:S(2)}, u32[]{:S(2)}) collective-permute-start(f32[2,8,128,128]{3,2,1,0:T(8,128)} %collective-permute-done.12), channel_id=1, source_target_pairs={{2,0},{3,1},{4,6},{5,7},{10,8},{11,9},{12,14},{13,15},{18,16},{19,... | collective-permute-start | bytes 3145736 | tf_op jit(solution)/shard_map/ppermute | solution.py:242
  48.8 114.8 %collective-permute-start.11 = (f32[2,8,128,128]{3,2,1,0:T(8,128)}, f32[2,8,128,128]{3,2,1,0:T(8,128)}, u32[]{:S(2)}, u32[]{:S(2)}) collective-permute-start(f32[2,8,128,128]{3,2,1,0:T(8,128)} %collective-permute-done.10), channel_id=1, source_target_pairs={{2,0},{3,1},{4,6},{5,7},{10,8},{11,9},{12,14},{13,15},{18,16},{19,... | collective-permute-start | bytes 3145736 | tf_op jit(solution)/shard_map/ppermute | solution.py:242
  130.1 54.7 %collective-permute-start.22 = (f32[2,8,128,128]{3,2,1,0:T(8,128)}, f32[2,8,128,128]{3,2,1,0:T(8,128)}, u32[]{:S(2)}, u32[]{:S(2)}) collective-permute-start(f32[2,8,128,128]{3,2,1,0:T(8,128)} %copy-done.3), channel_id=1, source_target_pairs={{0,16},{1,17},{2,18},{3,19},{4,20},{5,21},{6,22},{7,23},{8,24},{9,... | collective-permute-start | bytes 3145736 | tf_op jit(solution)/shard_map/ppermute | solution.py:242
  142.3 41.1 %collective-permute-start.5 = (f32[2,8,128,128]{3,2,1,0:T(8,128)}, f32[2,8,128,128]{3,2,1,0:T(8,128)}, u32[]{:S(2)}, u32[]{:S(2)}) collective-permute-start(f32[2,8,128,128]{3,2,1,0:T(8,128)} %pad_maximum_fusion.2), channel_id=1, source_target_pairs={{0,1},{1,0},{2,3},{3,2},{4,5},{5,4},{6,7},{7,6},{8,9},{9,8},{10,11... | collective-permute-start | bytes 3145736 | tf_op jit(solution)/shard_map/ppermute | solution.py:242
  142.3 42.6 %collective-permute-start.23 = (f32[2,8,128,128]{3,2,1,0:T(8,128)}, f32[2,8,128,128]{3,2,1,0:T(8,128)}, u32[]{:S(2)}, u32[]{:S(2)}) collective-permute-start(f32[2,8,128,128]{3,2,1,0:T(8,128)} %collective-permute-done.1), channel_id=1, source_target_pairs={{0,16},{1,17},{2,18},{3,19},{4,20},{5,21},{6,22},{7,23},{8,24},{9,... | collective-permute-start | bytes 3145736 | tf_op jit(solution)/shard_map/ppermute | solution.py:242
  144.1 24.8 %copy-start.5 = (f32[8,128,128]{2,1,0:T(8,128)S(1)}, f32[8,128,128]{2,1,0:T(8,128)}, u32[]{:S(2)}) copy-start(f32[8,128,128]{2,1,0:T(8,128)} %get-tuple-element.84) | copy-start | bytes 1572868
  144.1 35.2 %copy-start.4 = (f32[8,128,128]{2,1,0:T(8,128)S(1)}, f32[8,128,128]{2,1,0:T(8,128)}, u32[]{:S(2)}) copy-start(f32[8,128,128]{2,1,0:T(8,128)} %get-tuple-element.83) | copy-start | bytes 1572868
  144.4 24.5 %collective-permute-start.6 = (f32[8,128,128]{2,1,0:T(8,128)}, f32[8,128,128]{2,1,0:T(8,128)S(1)}, u32[]{:S(2)}, u32[]{:S(2)}) collective-permute-start(f32[8,128,128]{2,1,0:T(8,128)} %get-tuple-element.86), channel_id=1, source_target_pairs={{0,0},{1,8},{2,2},{3,10},{4,4},{5,12},{6,6},{7,14},{8,9},{9,1},{10... | collective-permute-start | bytes 1572872 | tf_op jit(solution)/shard_map/ppermute | solution.py:242
  163.6 15.7 %collective-permute-start.7 = (f32[8,128,128]{2,1,0:T(8,128)}, f32[8,128,128]{2,1,0:T(8,128)S(1)}, u32[]{:S(2)}, u32[]{:S(2)}) collective-permute-start(f32[8,128,128]{2,1,0:T(8,128)} %get-tuple-element.85), channel_id=1, source_target_pairs={{0,8},{1,0},{2,10},{3,2},{4,12},{5,4},{6,14},{7,6},{8,1},{9,9},{10... | collective-permute-start | bytes 1572872 | tf_op jit(solution)/shard_map/ppermute | solution.py:242
  168.9 19.3 %collective-permute-start.8 = (f32[8,128,128]{2,1,0:T(8,128)S(1)}, f32[8,128,128]{2,1,0:T(8,128)S(1)}, u32[]{:S(2)}, u32[]{:S(2)}) collective-permute-start(f32[8,128,128]{2,1,0:T(8,128)S(1)} %copy-done.5), channel_id=1, source_target_pairs={{0,2},{1,10},{2,0},{3,8},{4,6},{5,14},{6,4},{7,12},{8,11},{9,3},{1... | collective-permute-start | bytes 1572872 | tf_op jit(solution)/shard_map/ppermute | solution.py:242
  179.3 20.2 %collective-permute-start.9 = (f32[8,128,128]{2,1,0:T(8,128)S(1)}, f32[8,128,128]{2,1,0:T(8,128)S(1)}, u32[]{:S(2)}, u32[]{:S(2)}) collective-permute-start(f32[8,128,128]{2,1,0:T(8,128)S(1)} %copy-done.4), channel_id=1, source_target_pairs={{0,10},{1,2},{2,8},{3,0},{4,14},{5,6},{6,12},{7,4},{8,3},{9,11},{1... | collective-permute-start | bytes 1572872 | tf_op jit(solution)/shard_map/ppermute | solution.py:242
  183.3 26.3 %collective-permute-start.31 = (f32[2,8,128,128]{3,2,1,0:T(8,128)}, f32[2,8,128,128]{3,2,1,0:T(8,128)S(1)}, u32[]{:S(2)}, u32[]{:S(2)}) collective-permute-start(f32[2,8,128,128]{3,2,1,0:T(8,128)} %collective-permute-done.5.beside_ref.refs_3_), channel_id=1, source_target_pairs={{0,16},{1,17},{2,18},{3,19},{4,20},{5,21},{6,22},{7,23},{8,24},{9,... | collective-permute-start | bytes 3145736 | tf_op jit(solution)/shard_map/ppermute | solution.py:242
  184.8 36.5 %collective-permute-start.14 = (f32[2,8,128,128]{3,2,1,0:T(8,128)S(1)}, f32[2,8,128,128]{3,2,1,0:T(8,128)S(1)}, u32[]{:S(2)}, u32[]{:S(2)}) collective-permute-start(f32[2,8,128,128]{3,2,1,0:T(8,128)S(1)} %reverse_select_fusion), channel_id=1, source_target_pairs={{0,1},{1,0},{2,3},{3,2},{4,5},{5,4},{6,7},{7,6},{8,9},{9,8},{10,11... | collective-permute-start | bytes 3145736 | tf_op jit(solution)/shard_map/ppermute | solution.py:242
  184.8 46.0 %collective-permute-start.26 = (f32[2,8,128,128]{3,2,1,0:T(8,128)S(1)}, f32[2,8,128,128]{3,2,1,0:T(8,128)S(1)}, u32[]{:S(2)}, u32[]{:S(2)}) collective-permute-start(f32[2,8,128,128]{3,2,1,0:T(8,128)S(1)} %reverse_select_fusion.1.own_ref.refs_2_), channel_id=1, source_target_pairs={{0,16},{1,17},{2,18},{3,19},{4,20},{5,21},{6,22},{7,23},{8,24},{9,... | collective-permute-start | bytes 3145736 | tf_op jit(solution)/shard_map/ppermute | solution.py:242
  188.2 21.5 %collective-permute-start.18 = (f32[8,128,128]{2,1,0:T(8,128)S(1)}, f32[8,128,128]{2,1,0:T(8,128)S(1)}, u32[]{:S(2)}, u32[]{:S(2)}) collective-permute-start(f32[8,128,128]{2,1,0:T(8,128)S(1)} %get-tuple-element.79), channel_id=1, source_target_pairs={{0,14},{1,6},{2,12},{3,4},{4,10},{5,2},{6,8},{7,0},{8,7},{9,15},{1... | collective-permute-start | bytes 1572872 | tf_op jit(solution)/shard_map/ppermute | solution.py:242
  199.5 44.3 %collective-permute-start.24 = (f32[2,8,128,128]{3,2,1,0:T(8,128)S(1)}, f32[2,8,128,128]{3,2,1,0:T(8,128)S(1)}, u32[]{:S(2)}, u32[]{:S(2)}) collective-permute-start(f32[2,8,128,128]{3,2,1,0:T(8,128)S(1)} %pad_maximum_fusion.4.own_ref.refs_10_), channel_id=1, source_target_pairs={{0,1},{1,0},{2,3},{3,2},{4,5},{5,4},{6,7},{7,6},{8,9},{9,8},{10,11... | collective-permute-start | bytes 3145736 | tf_op jit(solution)/shard_map/ppermute | solution.py:242
  209.6 72.4 %collective-permute-start.19 = (f32[64,32,128]{2,1,0:T(8,128)S(1)}, f32[64,32,128]{2,1,0:T(8,128)S(1)}, u32[]{:S(2)}, u32[]{:S(2)}) collective-permute-start(f32[64,32,128]{2,1,0:T(8,128)S(1)} %get-tuple-element.47), channel_id=1, source_target_pairs={{0,8},{1,9},{2,10},{3,11},{4,12},{5,13},{6,14},{7,15},{8,0},{9,1},... | collective-permute-start | bytes 3145736 | tf_op jit(solution)/shard_map/ppermute | solution.py:242
  209.6 69.0 %collective-permute-start.25 = (f32[2,8,128,128]{3,2,1,0:T(8,128)S(1)}, f32[2,8,128,128]{3,2,1,0:T(8,128)S(1)}, u32[]{:S(2)}, u32[]{:S(2)}) collective-permute-start(f32[2,8,128,128]{3,2,1,0:T(8,128)S(1)} %reverse_select_fusion), channel_id=1, source_target_pairs={{0,16},{1,17},{2,18},{3,19},{4,20},{5,21},{6,22},{7,23},{8,24},{9,... | collective-permute-start | bytes 3145736 | tf_op jit(solution)/shard_map/ppermute | solution.py:242
  221.3 54.4 %collective-permute-start.32 = (f32[2,8,128,128]{3,2,1,0:T(8,128)S(1)}, f32[2,8,128,128]{3,2,1,0:T(8,128)S(1)}, u32[]{:S(2)}, u32[]{:S(2)}) collective-permute-start(f32[2,8,128,128]{3,2,1,0:T(8,128)S(1)} %collective-permute-done.14.beside_ref.refs_3_), channel_id=1, source_target_pairs={{0,16},{1,17},{2,18},{3,19},{4,20},{5,21},{6,22},{7,23},{8,24},{9,... | collective-permute-start | bytes 3145736 | tf_op jit(solution)/shard_map/ppermute | solution.py:242
  230.8 47.9 %collective-permute-start.27 = (f32[2,8,128,128]{3,2,1,0:T(8,128)S(1)}, f32[2,8,128,128]{3,2,1,0:T(8,128)S(1)}, u32[]{:S(2)}, u32[]{:S(2)}) collective-permute-start(f32[2,8,128,128]{3,2,1,0:T(8,128)S(1)} %collective-permute-done.26.own_ref.refs_10_), channel_id=1, source_target_pairs={{0,1},{1,0},{2,3},{3,2},{4,5},{5,4},{6,7},{7,6},{8,9},{9,8},{10,11... | collective-permute-start | bytes 3145736 | tf_op jit(solution)/shard_map/ppermute | solution.py:242
  243.8 39.7 %collective-permute-start.20 = (f32[64,32,128]{2,1,0:T(8,128)S(1)}, f32[64,32,128]{2,1,0:T(8,128)S(1)}, u32[]{:S(2)}, u32[]{:S(2)}) collective-permute-start(f32[64,32,128]{2,1,0:T(8,128)S(1)} %get-tuple-element.48), channel_id=1, source_target_pairs={{0,8},{1,9},{2,10},{3,11},{4,12},{5,13},{6,14},{7,15},{8,0},{9,1},... | collective-permute-start | bytes 3145736 | tf_op jit(solution)/shard_map/ppermute | solution.py:242
  275.8 10.8 %collective-permute-start.33 = (f32[64,32,128]{2,1,0:T(8,128)S(1)}, f32[64,32,128]{2,1,0:T(8,128)S(1)}, u32[]{:S(2)}, u32[]{:S(2)}) collective-permute-start(f32[64,32,128]{2,1,0:T(8,128)S(1)} %get-tuple-element.59), channel_id=1, source_target_pairs={{0,8},{1,9},{2,10},{3,11},{4,12},{5,13},{6,14},{7,15},{8,0},{9,1},... | collective-permute-start | bytes 3145736 | tf_op jit(solution)/shard_map/ppermute | solution.py:242
  278.6 10.6 %collective-permute-start.28 = (f32[64,32,128]{2,1,0:T(8,128)S(1)}, f32[64,32,128]{2,1,0:T(8,128)S(1)}, u32[]{:S(2)}, u32[]{:S(2)}) collective-permute-start(f32[64,32,128]{2,1,0:T(8,128)S(1)} %get-tuple-element.53), channel_id=1, source_target_pairs={{0,8},{1,9},{2,10},{3,11},{4,12},{5,13},{6,14},{7,15},{8,0},{9,1},... | collective-permute-start | bytes 3145736 | tf_op jit(solution)/shard_map/ppermute | solution.py:242
  278.7 7.8 %collective-permute-start.34 = (f32[64,32,128]{2,1,0:T(8,128)S(1)}, f32[64,32,128]{2,1,0:T(8,128)S(1)}, u32[]{:S(2)}, u32[]{:S(2)}) collective-permute-start(f32[64,32,128]{2,1,0:T(8,128)S(1)} %get-tuple-element.60), channel_id=1, source_target_pairs={{0,8},{1,9},{2,10},{3,11},{4,12},{5,13},{6,14},{7,15},{8,0},{9,1},... | collective-permute-start | bytes 3145736 | tf_op jit(solution)/shard_map/ppermute | solution.py:242
  282.0 7.2 %collective-permute-start.29 = (f32[64,32,128]{2,1,0:T(8,128)}, f32[64,32,128]{2,1,0:T(8,128)S(1)}, u32[]{:S(2)}, u32[]{:S(2)}) collective-permute-start(f32[64,32,128]{2,1,0:T(8,128)} %get-tuple-element.54), channel_id=1, source_target_pairs={{0,8},{1,9},{2,10},{3,11},{4,12},{5,13},{6,14},{7,15},{8,0},{9,1},... | collective-permute-start | bytes 3145736 | tf_op jit(solution)/shard_map/ppermute | solution.py:242
  286.0 6.7 %collective-permute-start.21 = (f32[64,32,128]{2,1,0:T(8,128)S(1)}, f32[64,32,128]{2,1,0:T(8,128)S(1)}, u32[]{:S(2)}, u32[]{:S(2)}) collective-permute-start(f32[64,32,128]{2,1,0:T(8,128)S(1)} %get-tuple-element.50), channel_id=1, source_target_pairs={{0,8},{1,9},{2,10},{3,11},{4,12},{5,13},{6,14},{7,15},{8,0},{9,1},... | collective-permute-start | bytes 3145736 | tf_op jit(solution)/shard_map/ppermute | solution.py:242
  289.1 3.8 collective-permute-start.35
  291.8 2.8 collective-permute-start.30
  292.3 7.6 %collective-permute-start.40 = (f32[64,32,128]{2,1,0:T(8,128)S(1)}, f32[64,32,128]{2,1,0:T(8,128)S(1)}, u32[]{:S(2)}, u32[]{:S(2)}) collective-permute-start(f32[64,32,128]{2,1,0:T(8,128)S(1)} %get-tuple-element.68), channel_id=1, source_target_pairs={{0,8},{1,9},{2,10},{3,11},{4,12},{5,13},{6,14},{7,15},{8,0},{9,1},... | collective-permute-start | bytes 3145736 | tf_op jit(solution)/shard_map/ppermute | solution.py:242
  292.3 7.8 %collective-permute-start.42 = (f32[64,32,128]{2,1,0:T(8,128)S(1)}, f32[64,32,128]{2,1,0:T(8,128)S(1)}, u32[]{:S(2)}, u32[]{:S(2)}) collective-permute-start(f32[64,32,128]{2,1,0:T(8,128)S(1)} %get-tuple-element.72), channel_id=1, source_target_pairs={{0,8},{1,9},{2,10},{3,11},{4,12},{5,13},{6,14},{7,15},{8,0},{9,1},... | collective-permute-start | bytes 3145736 | tf_op jit(solution)/shard_map/ppermute | solution.py:242
  292.8 7.4 %collective-permute-start.41 = (f32[64,32,128]{2,1,0:T(8,128)S(1)}, f32[64,32,128]{2,1,0:T(8,128)S(1)}, u32[]{:S(2)}, u32[]{:S(2)}) collective-permute-start(f32[64,32,128]{2,1,0:T(8,128)S(1)} %get-tuple-element.70), channel_id=1, source_target_pairs={{0,8},{1,9},{2,10},{3,11},{4,12},{5,13},{6,14},{7,15},{8,0},{9,1},... | collective-permute-start | bytes 3145736 | tf_op jit(solution)/shard_map/ppermute | solution.py:242
  299.7 56.0 %collective-permute-start.36 = (f32[8,128,128]{2,1,0:T(8,128)S(1)}, f32[8,128,128]{2,1,0:T(8,128)S(1)}, u32[]{:S(2)}, u32[]{:S(2)}) collective-permute-start(f32[8,128,128]{2,1,0:T(8,128)S(1)} %get-tuple-element.63), channel_id=1, source_target_pairs={{0,4},{1,13},{2,6},{3,15},{4,0},{5,9},{6,2},{7,11},{8,5},{9,12},{1... | collective-permute-start | bytes 1572872 | tf_op jit(solution)/shard_map/ppermute | solution.py:242
  299.8 65.8 %collective-permute-start.37 = (f32[8,128,128]{2,1,0:T(8,128)S(1)}, f32[8,128,128]{2,1,0:T(8,128)S(1)}, u32[]{:S(2)}, u32[]{:S(2)}) collective-permute-start(f32[8,128,128]{2,1,0:T(8,128)S(1)} %get-tuple-element.64), channel_id=1, source_target_pairs={{0,5},{1,12},{2,7},{3,14},{4,1},{5,8},{6,3},{7,10},{8,4},{9,13},{1... | collective-permute-start | bytes 1572872 | tf_op jit(solution)/shard_map/ppermute | solution.py:242
  299.9 67.5 %collective-permute-start.38 = (f32[8,128,128]{2,1,0:T(8,128)S(1)}, f32[8,128,128]{2,1,0:T(8,128)S(1)}, u32[]{:S(2)}, u32[]{:S(2)}) collective-permute-start(f32[8,128,128]{2,1,0:T(8,128)S(1)} %get-tuple-element.65), channel_id=1, source_target_pairs={{0,6},{1,15},{2,4},{3,13},{4,2},{5,11},{6,0},{7,9},{8,7},{9,14},{1... | collective-permute-start | bytes 1572872 | tf_op jit(solution)/shard_map/ppermute | solution.py:242
  300.2 57.6 %copy-start.2 = (f32[4,16,128,128]{3,2,1,0:T(8,128)S(1)}, f32[4,16,128,128]{3,2,1,0:T(8,128)}, u32[]{:S(2)}) copy-start(f32[4,16,128,128]{3,2,1,0:T(8,128)} %param.5) | copy-start | bytes 12582916
  300.2 67.1 %copy-start = (f32[4,16,128,128]{3,2,1,0:T(8,128)S(1)}, f32[4,16,128,128]{3,2,1,0:T(8,128)}, u32[]{:S(2)}) copy-start(f32[4,16,128,128]{3,2,1,0:T(8,128)} %param.5) | copy-start | bytes 12582916
  306.0 72.5 %collective-permute-start.43 = (f32[8,128,128]{2,1,0:T(8,128)S(1)}, f32[8,128,128]{2,1,0:T(8,128)S(1)}, u32[]{:S(2)}, u32[]{:S(2)}) collective-permute-start(f32[8,128,128]{2,1,0:T(8,128)S(1)} %get-tuple-element.73), channel_id=1, source_target_pairs={{0,0},{1,9},{2,2},{3,11},{4,4},{5,13},{6,6},{7,15},{8,1},{9,8},{10... | collective-permute-start | bytes 1572872 | tf_op jit(solution)/shard_map/ppermute | solution.py:242
  306.7 71.7 %collective-permute-start.39 = (f32[8,128,128]{2,1,0:T(8,128)S(1)}, f32[8,128,128]{2,1,0:T(8,128)S(1)}, u32[]{:S(2)}, u32[]{:S(2)}) collective-permute-start(f32[8,128,128]{2,1,0:T(8,128)S(1)} %get-tuple-element.66), channel_id=1, source_target_pairs={{0,7},{1,14},{2,5},{3,12},{4,3},{5,10},{6,1},{7,8},{8,6},{9,15},{1... | collective-permute-start | bytes 1572872 | tf_op jit(solution)/shard_map/ppermute | solution.py:242
  355.7 22.9 %collective-permute-start.44 = (f32[8,128,128]{2,1,0:T(8,128)S(1)}, f32[8,128,128]{2,1,0:T(8,128)S(1)}, u32[]{:S(2)}, u32[]{:S(2)}) collective-permute-start(f32[8,128,128]{2,1,0:T(8,128)S(1)} %get-tuple-element.74), channel_id=1, source_target_pairs={{0,1},{1,8},{2,3},{3,10},{4,5},{5,12},{6,7},{7,14},{8,0},{9,9},{10... | collective-permute-start | bytes 1572872 | tf_op jit(solution)/shard_map/ppermute | solution.py:242
  365.6 13.1 %collective-permute-start.45 = (f32[8,128,128]{2,1,0:T(8,128)S(1)}, f32[8,128,128]{2,1,0:T(8,128)S(1)}, u32[]{:S(2)}, u32[]{:S(2)}) collective-permute-start(f32[8,128,128]{2,1,0:T(8,128)S(1)} %get-tuple-element.75), channel_id=1, source_target_pairs={{0,2},{1,11},{2,0},{3,9},{4,6},{5,15},{6,4},{7,13},{8,3},{9,10},{1... | collective-permute-start | bytes 1572872 | tf_op jit(solution)/shard_map/ppermute | solution.py:242
  367.4 24.3 %collective-permute-start.46 = (f32[8,128,128]{2,1,0:T(8,128)S(1)}, f32[8,128,128]{2,1,0:T(8,128)S(1)}, u32[]{:S(2)}, u32[]{:S(2)}) collective-permute-start(f32[8,128,128]{2,1,0:T(8,128)S(1)} %get-tuple-element.76), channel_id=1, source_target_pairs={{0,3},{1,10},{2,1},{3,8},{4,7},{5,14},{6,5},{7,12},{8,2},{9,11},{1... | collective-permute-start | bytes 1572872 | tf_op jit(solution)/shard_map/ppermute | solution.py:242
  378.8 12.8 %copy-start.1 = (f32[4,16,128,128]{3,2,1,0:T(8,128)}, f32[4,16,128,128]{3,2,1,0:T(8,128)S(1)}, u32[]{:S(2)}) copy-start(f32[4,16,128,128]{3,2,1,0:T(8,128)S(1)} %fusion.1) | copy-start | bytes 12582916
where the time goes:
time: 393 us
  waiting for transfers between devices  271 us (69%)
  starting transfers between devices  65.2 us (17%)
  Pallas kernels  31.7 us (8%)
  other arithmetic  14.4 us (4%)
  local copies, waits for them, and re-layouts  9.89 us (3%)
    ppermute x47, waiting for transfers between devices, moved(): return lax.ppermute(value, AXES, pairs)  271 us
    ppermute x47, starting transfers between devices, moved(): return lax.ppermute(value, AXES, pairs)  65.2 us
    pallas_call x6, Pallas kernels, forward(): pl.pallas_call(forward_kernel, out_shape=(spectrum_shape, spectrum_shape)...  13.1 us
    pallas_call x2, Pallas kernels, inverse(): pl.pallas_call(inverse_kernel, out_shape=(piece_shape,) * 4, in_specs=sme...  11 us
  transfers between devices with their start and end apart: 47, of which 19 were waited for; matrix products, arithmetic and copies ran while one was open for 5% of the time, Pallas kernels for 8%

commit v1 on v0

--- a/solution.py
+++ b/solution.py
@@ -1,3 +1,4 @@
+import functools
 import math
 
 import jax
@@ -174,11 +175,17 @@
             out[row + 1] = lines[index * depth : (index + 1) * depth, width:]
 
 
-def inverse_kernel(flag_ref, weight_ref, right_ref, left_ref, *refs):
-    outs = refs[-4:]
-    groups = [refs[4 * index : 4 * index + 4] for index in range(len(refs) // 4 - 1)]
-    places, depth, extent, width = groups[0][2].shape
+def inverse_kernel(chosen, flag_ref, cross_ref, a_ref, b_ref, c_ref, d_ref, right_ref, left_ref, *refs):
+    outs = refs[-2 * len(chosen) :]
+    groups = [refs[4 * index : 4 * index + 4] for index in range((len(refs) - len(outs)) // 4)]
+    _, depth, extent, width = groups[0][2].shape
     flip = flag_ref[0] == 1
+    crossed = cross_ref[0] == 1
+    weights = (
+        jnp.where(crossed, a_ref[0], b_ref[0]),
+        jnp.where(crossed, d_ref[0], c_ref[0]),
+        jnp.where(crossed, c_ref[0], d_ref[0]),
+    )
 
     def potentials(own_ref, other_ref, slot):
         at = slice(slot * depth, (slot + 1) * depth)
@@ -193,18 +200,18 @@
             made += [both[:, :width], both[:, width:]]
         return made
 
-    for place in range(places):
+    for number, place in enumerate(chosen):
         sums = [[None] * depth, [None] * depth]
         for e in range(2):
             for index, (own_ref, other_ref, near_ref, beside_ref) in enumerate(groups):
                 made = potentials(own_ref, other_ref, 2 * place + e)
                 visitor = (near_ref, beside_ref)[e]
                 for p in range(depth):
-                    term = weight_ref[index] * visitor[place, p] * made[p]
+                    term = weights[index] * visitor[place, p] * made[p]
                     sums[e][p] = term if index == 0 else sums[e][p] + term
         for p in range(depth):
-            outs[2 * place][p] = jnp.where(flip, sums[1][p], sums[0][p])
-            outs[2 * place + 1][p] = jnp.where(flip, sums[0][p], sums[1][p])
+            outs[2 * number][p] = jnp.where(flip, sums[1][p], sums[0][p])
+            outs[2 * number + 1][p] = jnp.where(flip, sums[0][p], sums[1][p])
 
 
 def vmem(count):
@@ -264,19 +271,21 @@
     def shares(bits):
         return moved(occupations[0:1], lambda x, c, z, y: (x ^ (bits // 2), c ^ (bits % 2), z, y))
 
-    all_shares = jnp.concatenate([occupations[0:1]] + [shares(bits) for bits in range(1, bands)])
-
-    def share(x_bit, owner):
-        return lax.dynamic_slice(all_shares, (x_bit * 2 + (core ^ owner),), (1,))
+    all_shares = [occupations[0:1]] + [shares(bits) for bits in range(1, bands)]
 
     held = [[None, None] for _ in range(lines)]
+    middle = (line == 1) | (line == 2)
 
     def fetch(m, t):
-        held[m][t] = moved(
-            piece(line ^ m, core ^ side ^ t), lambda x, c, z, y: (x, c ^ y ^ t, z ^ m, c)
-        )
-
-    weights = jnp.concatenate([share(0, 1 - side), share(1, side), share(1, 1 - side)])
+        value = piece(line ^ m, core ^ side ^ t)
+        to = lambda x, c, z, y: (x, c ^ y ^ t, z ^ m, c)
+        if m < 3:
+            held[m][t] = moved(value, to)
+            return
+        inside = moved(value, lambda x, c, z, y: to(x, c, z, y) if z in (1, 2) else None)
+        outside = moved(value, lambda x, c, z, y: to(x, c, z, y) if z in (0, 3) else None)
+        held[m][t] = jnp.where(middle, inside, outside)
+
     orbitals, leads = lax.optimization_barrier((orbitals, leads))
     for m in range(lines):
         for t in range(2):
@@ -284,11 +293,9 @@
 
     leads_z = moved(leads, over_z)
     far_x = [moved(leads, over_x), moved(leads_z, over_x)]
-    leads_z, weights = lax.optimization_barrier((leads_z, weights))
     near = [jnp.stack([leads[row], leads_z[row]]) for row in range(2)]
     inner = [moved(near[row], over_middle) for row in range(2)]
     beside_near = moved(near[0], over_y)
-    middle = (line == 1) | (line == 2)
     outer = [moved(inner[row], outward) for row in range(2)]
     far = [jnp.where(middle, inner[row][::-1], outer[row]) for row in range(2)]
     x_near = [jnp.stack([far_x[0][row], far_x[1][row]]) for row in range(2)]
@@ -331,6 +338,7 @@
     screen = 4.0 * math.pi / (square + 0.01) / float(extent**3)
 
     flag = core.reshape(1).astype(jnp.int32)
+    cross = (core ^ side).reshape(1).astype(jnp.int32)
     group = lines // 2 * 2 * depth
     spectrum_shape = jax.ShapeDtypeStruct((keep, group, width), jnp.float32)
     piece_shape = jax.ShapeDtypeStruct((depth, extent, width), jnp.float32)
@@ -357,18 +365,18 @@
             name="across",
         )(*parts, screen, left_x_forth, left_x_back)
 
-    def inverse(part, spectra):
+    def inverse(part, chosen, spectra):
         operands = []
         for index, pair in enumerate(spectra):
             operands += [*pair, *visitors[index][part]]
         return pl.pallas_call(
-            inverse_kernel,
-            out_shape=(piece_shape,) * 4,
-            in_specs=smem(2) + vmem(len(operands) + 2),
-            out_specs=tuple(vmem(4)),
+            functools.partial(inverse_kernel, chosen),
+            out_shape=(piece_shape,) * (2 * len(chosen)),
+            in_specs=smem(2 + bands) + vmem(len(operands) + 2),
+            out_specs=tuple(vmem(2 * len(chosen))),
             compiler_params=params,
             name="inverse",
-        )(flag, weights, right, left_b_back, *operands)
+        )(flag, cross, *all_shares, right, left_b_back, *operands)
 
     spectra = [[], []]
     for index in range(HOPS):
@@ -382,15 +390,12 @@
             spectra[part].append((out[part], moved(out[2 + part], over_core)))
 
     result = accumulated
-    for part in (1, 0):
-        terms = inverse(part, spectra[part])
-        for place in range(2):
+    for part, chosen in ((1, (0,)), (1, (1,)), (0, (0, 1))):
+        terms = inverse(part, chosen, spectra[part])
+        for number, place in enumerate(chosen):
             for t in range(2):
                 m = 2 * part + place
-                back = moved(
-                    terms[2 * place + t],
-                    lambda x, c, z, y: (x, y, z ^ m, c ^ y ^ t),
-                )
+                back = moved(terms[2 * number + t], lambda x, c, z, y: (x, y, z ^ m, c ^ y ^ t))
                 start = (line ^ m, (core ^ side ^ t) * depth, 0, 0)
                 old = lax.dynamic_slice(accumulated, start, (1, depth, extent, width))
                 result = lax.dynamic_update_slice(result, old - back[None], start)

time: 393 us -> 415 us (1.056)
  starting transfers between devices: 65.2 us -> 139 us
  waiting for transfers between devices: 271 us -> 215 us
  Pallas kernels: 31.7 us -> 39.2 us
    ppermute x47 -> x49, starting transfers between devices: 65.2 us -> 139 us  [moved(): return lax.ppermute(value, AXES, pairs)]
    ppermute x47 -> x49, waiting for transfers between devices: 271 us -> 215 us  [moved(): return lax.ppermute(value, AXES, pairs)]
    pallas_call x2 -> x3, Pallas kernels: 11 us -> 15.7 us  [inverse(): pl.pallas_call(functools.partial(inverse_kernel, chosen), out_shape=(piec...]
  transfers between devices with their start and end apart: 47 -> 49, of which waited for: 19 -> 19; matrix products, arithmetic and copies ran while one was open for 5% -> 4% of each run, Pallas kernels for 8% -> 9%
where the time goes in v1:
time: 415 us
  waiting for transfers between devices  215 us (52%)
  starting transfers between devices  139 us (33%)
  Pallas kernels  39.2 us (9%)
  other arithmetic  11.6 us (3%)
  local copies, waits for them, and re-layouts  9.31 us (2%)
    ppermute x49, waiting for transfers between devices, moved(): return lax.ppermute(value, AXES, pairs)  215 us
    ppermute x49, starting transfers between devices, moved(): return lax.ppermute(value, AXES, pairs)  139 us
    pallas_call x3, Pallas kernels, inverse(): pl.pallas_call(functools.partial(inverse_kernel, chosen), out_shape=(piec...  15.7 us
    pallas_call x6, Pallas kernels, forward(): pl.pallas_call(forward_kernel, out_shape=(spectrum_shape, spectrum_shape)...  14 us
    pallas_call x3, Pallas kernels, across(): pl.pallas_call(across_kernel, out_shape=(spectrum_shape,) * 4, in_specs=v...  9.57 us
  transfers between devices with their start and end apart: 49, of which 19 were waited for; matrix products, arithmetic and copies ran while one was open for 4% of the time, Pallas kernels for 9%

profile of v1, /device:TPU:0, one launch (start us, length us, event | category | flops | bytes accessed | tf_op | source)
XLA Modules:
  0.0 414.7 jit_solution(13659542423521849491)
XLA Ops:
  1.6 1.5 collective-permute-done.3
  3.2 1.1 fusion.8
  5.4 2.9 collective-permute-start.4
  8.3 1.3 fusion.66
  9.6 22.4 %collective-permute-done.4 = f32[2,8,128,128]{3,2,1,0:T(8,128)S(1)} collective-permute-done((f32[2,8,128,128]{3,2,1,0:T(8,128)}, f32[2,8,128,128]{3,2,1,0:T(8,128)S(1)}, u32[]{:S(2)}, u32[]{:S(2)}) %collective-permute-start.4) | collective-permute-done | bytes 1048608 | tf_op jit(solution)/shard_map/ppermute | solution.py:249
  32.2 1.6 collective-permute-start.12
  33.9 1.7 collective-permute-start.10
  35.6 4.0 dynamic-slice_bitcast_fusion
  40.2 4.6 %collective-permute-start.20 = (f32[8,128,128]{2,1,0:T(8,128)S(1)}, f32[8,128,128]{2,1,0:T(8,128)S(1)}, u32[]{:S(2)}, u32[]{:S(2)}) collective-permute-start(f32[8,128,128]{2,1,0:T(8,128)S(1)} %get-tuple-element.75), channel_id=1, source_target_pairs={{0,14},{1,6},{6,8},{7,0},{8,7},{9,15},{14,1},{15,9},{16,30},{17,22... | collective-permute-start | bytes 1572872 | tf_op jit(solution)/shard_map/ppermute | solution.py:249
  44.8 1.5 collective-permute-start.17
  46.3 3.0 collective-permute-start.18
  49.3 10.4 %collective-permute-done.20 = f32[8,128,128]{2,1,0:T(8,128)S(1)} collective-permute-done((f32[8,128,128]{2,1,0:T(8,128)S(1)}, f32[8,128,128]{2,1,0:T(8,128)S(1)}, u32[]{:S(2)}, u32[]{:S(2)}) %collective-permute-start.20) | collective-permute-done | bytes 524320 | tf_op jit(solution)/shard_map/ppermute | solution.py:249
  59.7 61.8 %collective-permute-start.15 = (f32[8,128,128]{2,1,0:T(8,128)}, f32[8,128,128]{2,1,0:T(8,128)S(1)}, u32[]{:S(2)}, u32[]{:S(2)}) collective-permute-start(f32[8,128,128]{2,1,0:T(8,128)} %get-tuple-element.78), channel_id=1, source_target_pairs={{0,4},{1,12},{2,6},{3,14},{4,0},{5,8},{6,2},{7,10},{8,13},{9,5},{1... | collective-permute-start | bytes 1572872 | tf_op jit(solution)/shard_map/ppermute | solution.py:249
  121.5 1.3 collective-permute-start.13
  122.8 1.3 collective-permute-start.11
  124.7 1.6 collective-permute-start.24
  126.5 23.1 %collective-permute-done.15.refs_0_ = f32[8,128,128]{2,1,0:T(8,128)S(1)} collective-permute-done((f32[8,128,128]{2,1,0:T(8,128)}, f32[8,128,128]{2,1,0:T(8,128)S(1)}, u32[]{:S(2)}, u32[]{:S(2)}) %collective-permute-start.15) | collective-permute-done | bytes 524320 | tf_op jit(solution)/shard_map/ppermute | solution.py:249
  149.6 1.5 collective-permute-start.25
  151.8 9.2 %collective-permute-done.13 = f32[2,8,128,128]{3,2,1,0:T(8,128)} collective-permute-done((f32[2,8,128,128]{3,2,1,0:T(8,128)}, f32[2,8,128,128]{3,2,1,0:T(8,128)}, u32[]{:S(2)}, u32[]{:S(2)}) %collective-permute-start.13) | collective-permute-done | bytes 1048608 | tf_op jit(solution)/shard_map/ppermute | solution.py:249
  160.9 1.7 collective-permute-start.6
  162.6 16.2 %collective-permute-done.11 = f32[2,8,128,128]{3,2,1,0:T(8,128)} collective-permute-done((f32[2,8,128,128]{3,2,1,0:T(8,128)}, f32[2,8,128,128]{3,2,1,0:T(8,128)}, u32[]{:S(2)}, u32[]{:S(2)}) %collective-permute-start.11) | collective-permute-done | bytes 1048608 | tf_op jit(solution)/shard_map/ppermute | solution.py:249
  178.8 1.9 collective-permute-start.7
  180.8 1.7 reverse_select_fusion
  182.4 1.7 reverse_select_fusion.1.own_ref.refs_2_
  184.2 6.1 %collective-permute-done.7.refs_1_ = f32[8,128,128]{2,1,0:T(8,128)S(1)} collective-permute-done((f32[8,128,128]{2,1,0:T(8,128)}, f32[8,128,128]{2,1,0:T(8,128)S(1)}, u32[]{:S(2)}, u32[]{:S(2)}) %collective-permute-start.7) | collective-permute-done | bytes 524320 | tf_op jit(solution)/shard_map/ppermute | solution.py:249
  190.3 1.6 collective-permute-start.33
  191.9 6.8 %collective-permute-start.14 = (f32[2,8,128,128]{3,2,1,0:T(8,128)S(1)}, f32[2,8,128,128]{3,2,1,0:T(8,128)S(1)}, u32[]{:S(2)}, u32[]{:S(2)}) collective-permute-start(f32[2,8,128,128]{3,2,1,0:T(8,128)S(1)} %reverse_select_fusion), channel_id=1, source_target_pairs={{0,1},{1,0},{2,3},{3,2},{4,5},{5,4},{6,7},{7,6},{8,9},{9,8},{10,11... | collective-permute-start | bytes 3145736 | tf_op jit(solution)/shard_map/ppermute | solution.py:249
  199.2 1.3 fusion.64
  200.6 1.4 fusion.65
  202.3 15.3 %collective-permute-done.9.refs_3_ = f32[8,128,128]{2,1,0:T(8,128)S(1)} collective-permute-done((f32[8,128,128]{2,1,0:T(8,128)S(1)}, f32[8,128,128]{2,1,0:T(8,128)S(1)}, u32[]{:S(2)}, u32[]{:S(2)}) %collective-permute-start.9) | collective-permute-done | bytes 524320 | tf_op jit(solution)/shard_map/ppermute | solution.py:249
  218.2 1.8 forward.6
  220.0 7.1 %collective-permute-done.16.refs_1_ = f32[8,128,128]{2,1,0:T(8,128)S(1)} collective-permute-done((f32[8,128,128]{2,1,0:T(8,128)S(1)}, f32[8,128,128]{2,1,0:T(8,128)S(1)}, u32[]{:S(2)}, u32[]{:S(2)}) %collective-permute-start.16) | collective-permute-done | bytes 524320 | tf_op jit(solution)/shard_map/ppermute | solution.py:249
  228.0 1.5 collective-permute-start.27
  229.5 5.3 %collective-permute-done.14.beside_ref.refs_3_ = f32[2,8,128,128]{3,2,1,0:T(8,128)S(1)} collective-permute-done((f32[2,8,128,128]{3,2,1,0:T(8,128)S(1)}, f32[2,8,128,128]{3,2,1,0:T(8,128)S(1)}, u32[]{:S(2)}, u32[]{:S(2)}) %collective-permute-start.14) | collective-permute-done | bytes 1048608 | tf_op jit(solution)/shard_map/ppermute | solution.py:249
  235.8 3.2 collective-permute-start.29
  239.1 1.1 broadcast_select_fusion.1.refs_2_
  240.2 1.8 forward.7
  242.0 15.2 %collective-permute-done.26.beside_ref.refs_7_ = f32[2,8,128,128]{3,2,1,0:T(8,128)S(1)} collective-permute-done((f32[2,8,128,128]{3,2,1,0:T(8,128)S(1)}, f32[2,8,128,128]{3,2,1,0:T(8,128)S(1)}, u32[]{:S(2)}, u32[]{:S(2)}) %collective-permute-start.26) | collective-permute-done | bytes 1048608 | tf_op jit(solution)/shard_map/ppermute | solution.py:249
  257.4 2.8 forward.10
  260.3 1.8 forward.8
  262.1 18.3 %collective-permute-done.34.beside_ref.refs_11_ = f32[2,8,128,128]{3,2,1,0:T(8,128)S(1)} collective-permute-done((f32[2,8,128,128]{3,2,1,0:T(8,128)S(1)}, f32[2,8,128,128]{3,2,1,0:T(8,128)S(1)}, u32[]{:S(2)}, u32[]{:S(2)}) %collective-permute-start.34) | collective-permute-done | bytes 1048608 | tf_op jit(solution)/shard_map/ppermute | solution.py:249
  280.4 3.2 collective-permute-start.35
  283.7 2.8 forward.11
  287.0 2.8 forward.9
  289.9 1.4 divide_multiply_fusion.screen_ref
  291.3 3.5 across.3
  295.3 3.5 across.5
  298.9 2.5 across.4
  302.4 3.3 collective-permute-done.b_ref
  305.7 1.5 collective-permute-start.1
  307.2 2.2 collective-permute-done.1.c_ref
  309.5 2.8 collective-permute-done.2.d_ref
  312.9 4.2 %inverse.3 = (f32[8,128,128]{2,1,0:T(8,128)S(1)}, f32[8,128,128]{2,1,0:T(8,128)S(1)}) custom-call(s32[1]{0:T(128)} %bitcast.flag_ref, s32[1]{0:T(128)} %bitcast.1.cross_ref, f32[1]{0:T(128)S(1)} %bitcast.67, f32[1]{0:T(128)} %collective-permute-done.b_ref, f32[1]{0:T(128)} %collective-permute-done.1.c_ref, f32[1]{0:T(128)} %collective-permute-done.2.d_ref, ...), custom_call_target="tpu_custom_call" | custom-call | tf_op jit(solution)/shard_map/inverse/pallas_call | solution.py:372
  317.1 5.3 %collective-permute-start.38 = (f32[8,128,128]{2,1,0:T(8,128)S(1)}, f32[8,128,128]{2,1,0:T(8,128)S(1)}, u32[]{:S(2)}, u32[]{:S(2)}) collective-permute-start(f32[8,128,128]{2,1,0:T(8,128)S(1)} %get-tuple-element.59), channel_id=1, source_target_pairs={{0,4},{1,13},{2,6},{3,15},{4,0},{5,9},{6,2},{7,11},{8,5},{9,12},{1... | collective-permute-start | bytes 1572872 | tf_op jit(solution)/shard_map/ppermute | solution.py:249
  322.4 4.2 %inverse.4 = (f32[8,128,128]{2,1,0:T(8,128)S(1)}, f32[8,128,128]{2,1,0:T(8,128)S(1)}) custom-call(s32[1]{0:T(128)} %bitcast.flag_ref, s32[1]{0:T(128)} %bitcast.1.cross_ref, f32[1]{0:T(128)S(1)} %bitcast.68, f32[1]{0:T(128)} %collective-permute-done.b_ref, f32[1]{0:T(128)} %collective-permute-done.1.c_ref, f32[1]{0:T(128)} %collective-permute-done.2.d_ref, ...), custom_call_target="tpu_custom_call" | custom-call | tf_op jit(solution)/shard_map/inverse/pallas_call | solution.py:372
  326.6 3.1 collective-permute-start.40
  329.8 7.3 %inverse.5 = (f32[8,128,128]{2,1,0:T(8,128)S(1)}, f32[8,128,128]{2,1,0:T(8,128)S(1)}, f32[8,128,128]{2,1,0:T(8,128)S(1)}, f32[8,128,128]{2,1,0:T(8,128)S(1)}) custom-call(s32[1]{0:T(128)} %bitcast.flag_ref, s32[1]{0:T(128)} %bitcast.1.cross_ref, f32[1]{0:T(128)S(1)} %bitcast.69, f32[1]{0:T(128)} %collective-permute-done.b_ref, ...), custom_call_target="tpu_custom_call" | custom-call | tf_op jit(solution)/shard_map/inverse/pallas_call | solution.py:372
  337.7 3.1 collective-permute-start.41
  340.8 35.9 %collective-permute-done.38 = f32[8,128,128]{2,1,0:T(8,128)S(1)} collective-permute-done((f32[8,128,128]{2,1,0:T(8,128)S(1)}, f32[8,128,128]{2,1,0:T(8,128)S(1)}, u32[]{:S(2)}, u32[]{:S(2)}) %collective-permute-start.38) | collective-permute-done | bytes 524320 | tf_op jit(solution)/shard_map/ppermute | solution.py:249
  376.7 3.2 collective-permute-start.46
  380.1 7.7 %collective-permute-done.39 = f32[8,128,128]{2,1,0:T(8,128)S(1)} collective-permute-done((f32[8,128,128]{2,1,0:T(8,128)S(1)}, f32[8,128,128]{2,1,0:T(8,128)S(1)}, u32[]{:S(2)}, u32[]{:S(2)}) %collective-permute-start.39) | collective-permute-done | bytes 524320 | tf_op jit(solution)/shard_map/ppermute | solution.py:249
  387.9 12.6 %collective-permute-start.48 = (f32[8,128,128]{2,1,0:T(8,128)S(1)}, f32[8,128,128]{2,1,0:T(8,128)S(1)}, u32[]{:S(2)}, u32[]{:S(2)}) collective-permute-start(f32[8,128,128]{2,1,0:T(8,128)S(1)} %get-tuple-element.72), channel_id=1, source_target_pairs={{0,3},{1,10},{2,1},{3,8},{4,7},{5,14},{6,5},{7,12},{8,2},{9,11},{1... | collective-permute-start | bytes 1572872 | tf_op jit(solution)/shard_map/ppermute | solution.py:249
  400.9 1.3 collective-permute-done.47
  402.3 11.6 %collective-permute-done.48 = f32[8,128,128]{2,1,0:T(8,128)S(1)} collective-permute-done((f32[8,128,128]{2,1,0:T(8,128)S(1)}, f32[8,128,128]{2,1,0:T(8,128)S(1)}, u32[]{:S(2)}, u32[]{:S(2)}) %collective-permute-start.48) | collective-permute-done | bytes 524320 | tf_op jit(solution)/shard_map/ppermute | solution.py:249
  (113 shorter events, 13.8 us)
Async XLA Ops:
  1.1 2.1 collective-permute-start.3
  5.4 26.6 %collective-permute-start.4 = (f32[2,8,128,128]{3,2,1,0:T(8,128)}, f32[2,8,128,128]{3,2,1,0:T(8,128)S(1)}, u32[]{:S(2)}, u32[]{:S(2)}) collective-permute-start(f32[2,8,128,128]{3,2,1,0:T(8,128)} %pad_maximum_fusion), channel_id=1, source_target_pairs={{0,2},{1,3},{2,0},{3,1},{4,6},{5,7},{6,4},{7,5},{8,10},{9,11},{10,... | collective-permute-start | bytes 3145736 | tf_op jit(solution)/shard_map/ppermute | solution.py:249
  32.0 1.9 copy-start.4
  32.2 7.4 %copy-start.5 = (f32[2,8,128,128]{3,2,1,0:T(8,128)}, f32[2,8,128,128]{3,2,1,0:T(8,128)S(1)}, u32[]{:S(2)}) copy-start(f32[2,8,128,128]{3,2,1,0:T(8,128)S(1)} %pad_maximum_fusion.2) | copy-start | bytes 3145732
  32.2 89.3 %collective-permute-start.12 = (f32[2,8,128,128]{3,2,1,0:T(8,128)S(1)}, f32[2,8,128,128]{3,2,1,0:T(8,128)}, u32[]{:S(2)}, u32[]{:S(2)}) collective-permute-start(f32[2,8,128,128]{3,2,1,0:T(8,128)S(1)} %pad_maximum_fusion.2), channel_id=1, source_target_pairs={{2,4},{3,5},{4,2},{5,3},{10,12},{11,13},{12,10},{13,11},{18,20},{1... | collective-permute-start | bytes 3145736 | tf_op jit(solution)/shard_map/ppermute | solution.py:249
  33.9 88.9 %collective-permute-start.10 = (f32[2,8,128,128]{3,2,1,0:T(8,128)S(1)}, f32[2,8,128,128]{3,2,1,0:T(8,128)}, u32[]{:S(2)}, u32[]{:S(2)}) collective-permute-start(f32[2,8,128,128]{3,2,1,0:T(8,128)S(1)} %pad_maximum_fusion.1.own_ref.refs_2_), channel_id=1, source_target_pairs={{2,4},{3,5},{4,2},{5,3},{10,12},{11,13},{12,10},{13,11},{18,20},{1... | collective-permute-start | bytes 3145736 | tf_op jit(solution)/shard_map/ppermute | solution.py:249
  39.5 6.8 %collective-permute-start.19 = (f32[8,128,128]{2,1,0:T(8,128)S(1)}, f32[8,128,128]{2,1,0:T(8,128)S(1)}, u32[]{:S(2)}, u32[]{:S(2)}) collective-permute-start(f32[8,128,128]{2,1,0:T(8,128)S(1)} %get-tuple-element.75), channel_id=1, source_target_pairs={{2,12},{3,4},{4,10},{5,2},{10,5},{11,13},{12,3},{13,11},{18,28},{1... | collective-permute-start | bytes 1572872 | tf_op jit(solution)/shard_map/ppermute | solution.py:249
  40.2 19.5 %collective-permute-start.20 = (f32[8,128,128]{2,1,0:T(8,128)S(1)}, f32[8,128,128]{2,1,0:T(8,128)S(1)}, u32[]{:S(2)}, u32[]{:S(2)}) collective-permute-start(f32[8,128,128]{2,1,0:T(8,128)S(1)} %get-tuple-element.75), channel_id=1, source_target_pairs={{0,14},{1,6},{6,8},{7,0},{8,7},{9,15},{14,1},{15,9},{16,30},{17,22... | collective-permute-start | bytes 1572872 | tf_op jit(solution)/shard_map/ppermute | solution.py:249
  44.8 79.9 %collective-permute-start.17 = (f32[8,128,128]{2,1,0:T(8,128)}, f32[8,128,128]{2,1,0:T(8,128)}, u32[]{:S(2)}, u32[]{:S(2)}) collective-permute-start(f32[8,128,128]{2,1,0:T(8,128)} %get-tuple-element.76), channel_id=1, source_target_pairs={{2,4},{3,12},{4,2},{5,10},{10,13},{11,5},{12,11},{13,3},{18,20},{1... | collective-permute-start | bytes 1572872 | tf_op jit(solution)/shard_map/ppermute | solution.py:249
  46.3 76.5 %copy-start.8 = (f32[8,128,128]{2,1,0:T(8,128)}, f32[8,128,128]{2,1,0:T(8,128)S(1)}, u32[]{:S(2)}) copy-start(f32[8,128,128]{2,1,0:T(8,128)S(1)} %collective-permute-done.19) | copy-start | bytes 1572868
  46.3 80.0 %collective-permute-start.18 = (f32[8,128,128]{2,1,0:T(8,128)}, f32[8,128,128]{2,1,0:T(8,128)}, u32[]{:S(2)}, u32[]{:S(2)}) collective-permute-start(f32[8,128,128]{2,1,0:T(8,128)} %get-tuple-element.76), channel_id=1, source_target_pairs={{0,6},{1,14},{6,0},{7,8},{8,15},{9,7},{14,9},{15,1},{16,22},{17,30... | collective-permute-start | bytes 1572872 | tf_op jit(solution)/shard_map/ppermute | solution.py:249
  59.7 64.4 %copy-start.10 = (f32[8,128,128]{2,1,0:T(8,128)}, f32[8,128,128]{2,1,0:T(8,128)S(1)}, u32[]{:S(2)}) copy-start(f32[8,128,128]{2,1,0:T(8,128)S(1)} %collective-permute-done.20) | copy-start | bytes 1572868
  59.7 89.9 %collective-permute-start.15 = (f32[8,128,128]{2,1,0:T(8,128)}, f32[8,128,128]{2,1,0:T(8,128)S(1)}, u32[]{:S(2)}, u32[]{:S(2)}) collective-permute-start(f32[8,128,128]{2,1,0:T(8,128)} %get-tuple-element.78), channel_id=1, source_target_pairs={{0,4},{1,12},{2,6},{3,14},{4,0},{5,8},{6,2},{7,10},{8,13},{9,5},{1... | collective-permute-start | bytes 1572872 | tf_op jit(solution)/shard_map/ppermute | solution.py:249
  121.5 39.5 %collective-permute-start.13 = (f32[2,8,128,128]{3,2,1,0:T(8,128)}, f32[2,8,128,128]{3,2,1,0:T(8,128)}, u32[]{:S(2)}, u32[]{:S(2)}) collective-permute-start(f32[2,8,128,128]{3,2,1,0:T(8,128)} %collective-permute-done.12), channel_id=1, source_target_pairs={{2,0},{3,1},{4,6},{5,7},{10,8},{11,9},{12,14},{13,15},{18,16},{19,... | collective-permute-start | bytes 3145736 | tf_op jit(solution)/shard_map/ppermute | solution.py:249
  122.8 56.1 %collective-permute-start.11 = (f32[2,8,128,128]{3,2,1,0:T(8,128)}, f32[2,8,128,128]{3,2,1,0:T(8,128)}, u32[]{:S(2)}, u32[]{:S(2)}) collective-permute-start(f32[2,8,128,128]{3,2,1,0:T(8,128)} %collective-permute-done.10), channel_id=1, source_target_pairs={{2,0},{3,1},{4,6},{5,7},{10,8},{11,9},{12,14},{13,15},{18,16},{19,... | collective-permute-start | bytes 3145736 | tf_op jit(solution)/shard_map/ppermute | solution.py:249
  124.7 67.2 %collective-permute-start.24 = (f32[2,8,128,128]{3,2,1,0:T(8,128)}, f32[2,8,128,128]{3,2,1,0:T(8,128)}, u32[]{:S(2)}, u32[]{:S(2)}) collective-permute-start(f32[2,8,128,128]{3,2,1,0:T(8,128)} %pad_maximum_fusion), channel_id=1, source_target_pairs={{0,16},{1,17},{2,18},{3,19},{4,20},{5,21},{6,22},{7,23},{8,24},{9,... | collective-permute-start | bytes 3145736 | tf_op jit(solution)/shard_map/ppermute | solution.py:249
  126.3 64.1 %collective-permute-start.5 = (f32[2,8,128,128]{3,2,1,0:T(8,128)}, f32[2,8,128,128]{3,2,1,0:T(8,128)S(1)}, u32[]{:S(2)}, u32[]{:S(2)}) collective-permute-start(f32[2,8,128,128]{3,2,1,0:T(8,128)} %copy-done.5), channel_id=1, source_target_pairs={{0,1},{1,0},{2,3},{3,2},{4,5},{5,4},{6,7},{7,6},{8,9},{9,8},{10,11... | collective-permute-start | bytes 3145736 | tf_op jit(solution)/shard_map/ppermute | solution.py:249
  149.6 49.1 %collective-permute-start.25 = (f32[2,8,128,128]{3,2,1,0:T(8,128)}, f32[2,8,128,128]{3,2,1,0:T(8,128)}, u32[]{:S(2)}, u32[]{:S(2)}) collective-permute-start(f32[2,8,128,128]{3,2,1,0:T(8,128)} %copy-done.4), channel_id=1, source_target_pairs={{0,16},{1,17},{2,18},{3,19},{4,20},{5,21},{6,22},{7,23},{8,24},{9,... | collective-permute-start | bytes 3145736 | tf_op jit(solution)/shard_map/ppermute | solution.py:249
  151.1 33.0 %copy-start.7 = (f32[8,128,128]{2,1,0:T(8,128)S(1)}, f32[8,128,128]{2,1,0:T(8,128)}, u32[]{:S(2)}) copy-start(f32[8,128,128]{2,1,0:T(8,128)} %get-tuple-element.80) | copy-start | bytes 1572868
  151.1 39.2 %copy-start.6 = (f32[8,128,128]{2,1,0:T(8,128)S(1)}, f32[8,128,128]{2,1,0:T(8,128)}, u32[]{:S(2)}) copy-start(f32[8,128,128]{2,1,0:T(8,128)} %get-tuple-element.79) | copy-start | bytes 1572868
  160.9 23.2 %collective-permute-start.6 = (f32[8,128,128]{2,1,0:T(8,128)}, f32[8,128,128]{2,1,0:T(8,128)S(1)}, u32[]{:S(2)}, u32[]{:S(2)}) collective-permute-start(f32[8,128,128]{2,1,0:T(8,128)} %get-tuple-element.82), channel_id=1, source_target_pairs={{0,0},{1,8},{2,2},{3,10},{4,4},{5,12},{6,6},{7,14},{8,9},{9,1},{10... | collective-permute-start | bytes 1572872 | tf_op jit(solution)/shard_map/ppermute | solution.py:249
  178.8 11.5 %collective-permute-start.7 = (f32[8,128,128]{2,1,0:T(8,128)}, f32[8,128,128]{2,1,0:T(8,128)S(1)}, u32[]{:S(2)}, u32[]{:S(2)}) collective-permute-start(f32[8,128,128]{2,1,0:T(8,128)} %get-tuple-element.81), channel_id=1, source_target_pairs={{0,8},{1,0},{2,10},{3,2},{4,12},{5,4},{6,14},{7,6},{8,1},{9,9},{10... | collective-permute-start | bytes 1572872 | tf_op jit(solution)/shard_map/ppermute | solution.py:249
  184.1 17.9 %collective-permute-start.8 = (f32[8,128,128]{2,1,0:T(8,128)S(1)}, f32[8,128,128]{2,1,0:T(8,128)S(1)}, u32[]{:S(2)}, u32[]{:S(2)}) collective-permute-start(f32[8,128,128]{2,1,0:T(8,128)S(1)} %copy-done.7), channel_id=1, source_target_pairs={{0,2},{1,10},{2,0},{3,8},{4,6},{5,14},{6,4},{7,12},{8,11},{9,3},{1... | collective-permute-start | bytes 1572872 | tf_op jit(solution)/shard_map/ppermute | solution.py:249
  190.3 27.2 %collective-permute-start.9 = (f32[8,128,128]{2,1,0:T(8,128)S(1)}, f32[8,128,128]{2,1,0:T(8,128)S(1)}, u32[]{:S(2)}, u32[]{:S(2)}) collective-permute-start(f32[8,128,128]{2,1,0:T(8,128)S(1)} %copy-done.6), channel_id=1, source_target_pairs={{0,10},{1,2},{2,8},{3,0},{4,14},{5,6},{6,12},{7,4},{8,3},{9,11},{1... | collective-permute-start | bytes 1572872 | tf_op jit(solution)/shard_map/ppermute | solution.py:249
  190.3 37.7 %collective-permute-start.33 = (f32[2,8,128,128]{3,2,1,0:T(8,128)S(1)}, f32[2,8,128,128]{3,2,1,0:T(8,128)S(1)}, u32[]{:S(2)}, u32[]{:S(2)}) collective-permute-start(f32[2,8,128,128]{3,2,1,0:T(8,128)S(1)} %collective-permute-done.5.beside_ref.refs_3_), channel_id=1, source_target_pairs={{0,16},{1,17},{2,18},{3,19},{4,20},{5,21},{6,22},{7,23},{8,24},{9,... | collective-permute-start | bytes 3145736 | tf_op jit(solution)/shard_map/ppermute | solution.py:249
  191.9 42.8 %collective-permute-start.14 = (f32[2,8,128,128]{3,2,1,0:T(8,128)S(1)}, f32[2,8,128,128]{3,2,1,0:T(8,128)S(1)}, u32[]{:S(2)}, u32[]{:S(2)}) collective-permute-start(f32[2,8,128,128]{3,2,1,0:T(8,128)S(1)} %reverse_select_fusion), channel_id=1, source_target_pairs={{0,1},{1,0},{2,3},{3,2},{4,5},{5,4},{6,7},{7,6},{8,9},{9,8},{10,11... | collective-permute-start | bytes 3145736 | tf_op jit(solution)/shard_map/ppermute | solution.py:249
  198.7 37.1 %collective-permute-start.28 = (f32[2,8,128,128]{3,2,1,0:T(8,128)S(1)}, f32[2,8,128,128]{3,2,1,0:T(8,128)S(1)}, u32[]{:S(2)}, u32[]{:S(2)}) collective-permute-start(f32[2,8,128,128]{3,2,1,0:T(8,128)S(1)} %reverse_select_fusion.1.own_ref.refs_2_), channel_id=1, source_target_pairs={{0,16},{1,17},{2,18},{3,19},{4,20},{5,21},{6,22},{7,23},{8,24},{9,... | collective-permute-start | bytes 3145736 | tf_op jit(solution)/shard_map/ppermute | solution.py:249
  200.5 38.5 %copy-start.9 = (f32[8,128,128]{2,1,0:T(8,128)S(1)}, f32[8,128,128]{2,1,0:T(8,128)}, u32[]{:S(2)}) copy-start(f32[8,128,128]{2,1,0:T(8,128)} %copy-done.8) | copy-start | bytes 1572868
  200.5 38.5 %copy-start.11 = (f32[8,128,128]{2,1,0:T(8,128)S(1)}, f32[8,128,128]{2,1,0:T(8,128)}, u32[]{:S(2)}) copy-start(f32[8,128,128]{2,1,0:T(8,128)} %copy-done.10) | copy-start | bytes 1572868
  202.0 25.1 %collective-permute-start.16 = (f32[8,128,128]{2,1,0:T(8,128)S(1)}, f32[8,128,128]{2,1,0:T(8,128)S(1)}, u32[]{:S(2)}, u32[]{:S(2)}) collective-permute-start(f32[8,128,128]{2,1,0:T(8,128)S(1)} %get-tuple-element.77), channel_id=1, source_target_pairs={{0,12},{1,4},{2,14},{3,6},{4,8},{5,0},{6,10},{7,2},{8,5},{9,13},{1... | collective-permute-start | bytes 1572872 | tf_op jit(solution)/shard_map/ppermute | solution.py:249
  217.6 39.7 %collective-permute-start.26 = (f32[2,8,128,128]{3,2,1,0:T(8,128)S(1)}, f32[2,8,128,128]{3,2,1,0:T(8,128)S(1)}, u32[]{:S(2)}, u32[]{:S(2)}) collective-permute-start(f32[2,8,128,128]{3,2,1,0:T(8,128)S(1)} %pad_maximum_fusion.4.own_ref.refs_10_), channel_id=1, source_target_pairs={{0,1},{1,0},{2,3},{3,2},{4,5},{5,4},{6,7},{7,6},{8,9},{9,8},{10,11... | collective-permute-start | bytes 3145736 | tf_op jit(solution)/shard_map/ppermute | solution.py:249
  227.2 62.7 %collective-permute-start.21 = (f32[64,32,128]{2,1,0:T(8,128)S(1)}, f32[64,32,128]{2,1,0:T(8,128)S(1)}, u32[]{:S(2)}, u32[]{:S(2)}) collective-permute-start(f32[64,32,128]{2,1,0:T(8,128)S(1)} %get-tuple-element.43), channel_id=1, source_target_pairs={{0,8},{1,9},{2,10},{3,11},{4,12},{5,13},{6,14},{7,15},{8,0},{9,1},... | collective-permute-start | bytes 3145736 | tf_op jit(solution)/shard_map/ppermute | solution.py:249
  228.0 58.5 %collective-permute-start.27 = (f32[2,8,128,128]{3,2,1,0:T(8,128)S(1)}, f32[2,8,128,128]{3,2,1,0:T(8,128)S(1)}, u32[]{:S(2)}, u32[]{:S(2)}) collective-permute-start(f32[2,8,128,128]{3,2,1,0:T(8,128)S(1)} %reverse_select_fusion), channel_id=1, source_target_pairs={{0,16},{1,17},{2,18},{3,19},{4,20},{5,21},{6,22},{7,23},{8,24},{9,... | collective-permute-start | bytes 3145736 | tf_op jit(solution)/shard_map/ppermute | solution.py:249
  234.8 45.7 %collective-permute-start.34 = (f32[2,8,128,128]{3,2,1,0:T(8,128)S(1)}, f32[2,8,128,128]{3,2,1,0:T(8,128)S(1)}, u32[]{:S(2)}, u32[]{:S(2)}) collective-permute-start(f32[2,8,128,128]{3,2,1,0:T(8,128)S(1)} %collective-permute-done.14.beside_ref.refs_3_), channel_id=1, source_target_pairs={{0,16},{1,17},{2,18},{3,19},{4,20},{5,21},{6,22},{7,23},{8,24},{9,... | collective-permute-start | bytes 3145736 | tf_op jit(solution)/shard_map/ppermute | solution.py:249
  235.8 50.8 %collective-permute-start.29 = (f32[2,8,128,128]{3,2,1,0:T(8,128)S(1)}, f32[2,8,128,128]{3,2,1,0:T(8,128)S(1)}, u32[]{:S(2)}, u32[]{:S(2)}) collective-permute-start(f32[2,8,128,128]{3,2,1,0:T(8,128)S(1)} %collective-permute-done.28.own_ref.refs_10_), channel_id=1, source_target_pairs={{0,1},{1,0},{2,3},{3,2},{4,5},{5,4},{6,7},{7,6},{8,9},{9,8},{10,11... | collective-permute-start | bytes 3145736 | tf_op jit(solution)/shard_map/ppermute | solution.py:249
  257.2 34.1 %collective-permute-start.22 = (f32[64,32,128]{2,1,0:T(8,128)S(1)}, f32[64,32,128]{2,1,0:T(8,128)S(1)}, u32[]{:S(2)}, u32[]{:S(2)}) collective-permute-start(f32[64,32,128]{2,1,0:T(8,128)S(1)} %get-tuple-element.44), channel_id=1, source_target_pairs={{0,8},{1,9},{2,10},{3,11},{4,12},{5,13},{6,14},{7,15},{8,0},{9,1},... | collective-permute-start | bytes 3145736 | tf_op jit(solution)/shard_map/ppermute | solution.py:249
  280.4 14.8 %collective-permute-start.35 = (f32[64,32,128]{2,1,0:T(8,128)}, f32[64,32,128]{2,1,0:T(8,128)S(1)}, u32[]{:S(2)}, u32[]{:S(2)}) collective-permute-start(f32[64,32,128]{2,1,0:T(8,128)} %get-tuple-element.55), channel_id=1, source_target_pairs={{0,8},{1,9},{2,10},{3,11},{4,12},{5,13},{6,14},{7,15},{8,0},{9,1},... | collective-permute-start | bytes 3145736 | tf_op jit(solution)/shard_map/ppermute | solution.py:249
  286.5 12.3 %collective-permute-start.30 = (f32[64,32,128]{2,1,0:T(8,128)S(1)}, f32[64,32,128]{2,1,0:T(8,128)S(1)}, u32[]{:S(2)}, u32[]{:S(2)}) collective-permute-start(f32[64,32,128]{2,1,0:T(8,128)S(1)} %get-tuple-element.49), channel_id=1, source_target_pairs={{0,8},{1,9},{2,10},{3,11},{4,12},{5,13},{6,14},{7,15},{8,0},{9,1},... | collective-permute-start | bytes 3145736 | tf_op jit(solution)/shard_map/ppermute | solution.py:249
  286.5 8.7 %collective-permute-start.36 = (f32[64,32,128]{2,1,0:T(8,128)}, f32[64,32,128]{2,1,0:T(8,128)S(1)}, u32[]{:S(2)}, u32[]{:S(2)}) collective-permute-start(f32[64,32,128]{2,1,0:T(8,128)} %get-tuple-element.56), channel_id=1, source_target_pairs={{0,8},{1,9},{2,10},{3,11},{4,12},{5,13},{6,14},{7,15},{8,0},{9,1},... | collective-permute-start | bytes 3145736 | tf_op jit(solution)/shard_map/ppermute | solution.py:249
  289.8 9.0 %collective-permute-start.31 = (f32[64,32,128]{2,1,0:T(8,128)}, f32[64,32,128]{2,1,0:T(8,128)S(1)}, u32[]{:S(2)}, u32[]{:S(2)}) collective-permute-start(f32[64,32,128]{2,1,0:T(8,128)} %get-tuple-element.50), channel_id=1, source_target_pairs={{0,8},{1,9},{2,10},{3,11},{4,12},{5,13},{6,14},{7,15},{8,0},{9,1},... | collective-permute-start | bytes 3145736 | tf_op jit(solution)/shard_map/ppermute | solution.py:249
  294.8 17.5 %collective-permute-start.23 = (f32[64,32,128]{2,1,0:T(8,128)}, f32[64,32,128]{2,1,0:T(8,128)S(1)}, u32[]{:S(2)}, u32[]{:S(2)}) collective-permute-start(f32[64,32,128]{2,1,0:T(8,128)} %get-tuple-element.46), channel_id=1, source_target_pairs={{0,8},{1,9},{2,10},{3,11},{4,12},{5,13},{6,14},{7,15},{8,0},{9,1},... | collective-permute-start | bytes 3145736 | tf_op jit(solution)/shard_map/ppermute | solution.py:249
  298.8 14.1 %collective-permute-start.37 = (f32[64,32,128]{2,1,0:T(8,128)}, f32[64,32,128]{2,1,0:T(8,128)S(1)}, u32[]{:S(2)}, u32[]{:S(2)}) collective-permute-start(f32[64,32,128]{2,1,0:T(8,128)} %get-tuple-element.58), channel_id=1, source_target_pairs={{0,8},{1,9},{2,10},{3,11},{4,12},{5,13},{6,14},{7,15},{8,0},{9,1},... | collective-permute-start | bytes 3145736 | tf_op jit(solution)/shard_map/ppermute | solution.py:249
  298.9 3.1 copy-start
  301.4 11.5 %collective-permute-start.32 = (f32[64,32,128]{2,1,0:T(8,128)S(1)}, f32[64,32,128]{2,1,0:T(8,128)S(1)}, u32[]{:S(2)}, u32[]{:S(2)}) collective-permute-start(f32[64,32,128]{2,1,0:T(8,128)S(1)} %get-tuple-element.52), channel_id=1, source_target_pairs={{0,8},{1,9},{2,10},{3,11},{4,12},{5,13},{6,14},{7,15},{8,0},{9,1},... | collective-permute-start | bytes 3145736 | tf_op jit(solution)/shard_map/ppermute | solution.py:249
  301.9 24.7 %collective-permute-start.42 = (f32[64,32,128]{2,1,0:T(8,128)S(1)}, f32[64,32,128]{2,1,0:T(8,128)S(1)}, u32[]{:S(2)}, u32[]{:S(2)}) collective-permute-start(f32[64,32,128]{2,1,0:T(8,128)S(1)} %get-tuple-element.64), channel_id=1, source_target_pairs={{0,8},{1,9},{2,10},{3,11},{4,12},{5,13},{6,14},{7,15},{8,0},{9,1},... | collective-permute-start | bytes 3145736 | tf_op jit(solution)/shard_map/ppermute | solution.py:249
  302.0 3.7 collective-permute-start
  305.7 3.7 collective-permute-start.1
  309.4 2.9 collective-permute-start.2
  312.3 17.4 %collective-permute-start.44 = (f32[64,32,128]{2,1,0:T(8,128)S(1)}, f32[64,32,128]{2,1,0:T(8,128)S(1)}, u32[]{:S(2)}, u32[]{:S(2)}) collective-permute-start(f32[64,32,128]{2,1,0:T(8,128)S(1)} %get-tuple-element.68), channel_id=1, source_target_pairs={{0,8},{1,9},{2,10},{3,11},{4,12},{5,13},{6,14},{7,15},{8,0},{9,1},... | collective-permute-start | bytes 3145736 | tf_op jit(solution)/shard_map/ppermute | solution.py:249
  312.3 17.4 %collective-permute-start.43 = (f32[64,32,128]{2,1,0:T(8,128)S(1)}, f32[64,32,128]{2,1,0:T(8,128)S(1)}, u32[]{:S(2)}, u32[]{:S(2)}) collective-permute-start(f32[64,32,128]{2,1,0:T(8,128)S(1)} %get-tuple-element.66), channel_id=1, source_target_pairs={{0,8},{1,9},{2,10},{3,11},{4,12},{5,13},{6,14},{7,15},{8,0},{9,1},... | collective-permute-start | bytes 3145736 | tf_op jit(solution)/shard_map/ppermute | solution.py:249
  317.1 59.6 %collective-permute-start.38 = (f32[8,128,128]{2,1,0:T(8,128)S(1)}, f32[8,128,128]{2,1,0:T(8,128)S(1)}, u32[]{:S(2)}, u32[]{:S(2)}) collective-permute-start(f32[8,128,128]{2,1,0:T(8,128)S(1)} %get-tuple-element.59), channel_id=1, source_target_pairs={{0,4},{1,13},{2,6},{3,15},{4,0},{5,9},{6,2},{7,11},{8,5},{9,12},{1... | collective-permute-start | bytes 1572872 | tf_op jit(solution)/shard_map/ppermute | solution.py:249
  322.4 65.5 %collective-permute-start.39 = (f32[8,128,128]{2,1,0:T(8,128)S(1)}, f32[8,128,128]{2,1,0:T(8,128)S(1)}, u32[]{:S(2)}, u32[]{:S(2)}) collective-permute-start(f32[8,128,128]{2,1,0:T(8,128)S(1)} %get-tuple-element.60), channel_id=1, source_target_pairs={{0,5},{1,12},{2,7},{3,14},{4,1},{5,8},{6,3},{7,10},{8,4},{9,13},{1... | collective-permute-start | bytes 1572872 | tf_op jit(solution)/shard_map/ppermute | solution.py:249
  326.6 61.3 %collective-permute-start.40 = (f32[8,128,128]{2,1,0:T(8,128)S(1)}, f32[8,128,128]{2,1,0:T(8,128)S(1)}, u32[]{:S(2)}, u32[]{:S(2)}) collective-permute-start(f32[8,128,128]{2,1,0:T(8,128)S(1)} %get-tuple-element.61), channel_id=1, source_target_pairs={{0,6},{1,15},{2,4},{3,13},{4,2},{5,11},{6,0},{7,9},{8,7},{9,14},{1... | collective-permute-start | bytes 1572872 | tf_op jit(solution)/shard_map/ppermute | solution.py:249
  329.7 50.2 %copy-start.3 = (f32[4,16,128,128]{3,2,1,0:T(8,128)S(1)}, f32[4,16,128,128]{3,2,1,0:T(8,128)}, u32[]{:S(2)}) copy-start(f32[4,16,128,128]{3,2,1,0:T(8,128)} %param.5) | copy-start | bytes 12582916
  329.7 58.1 %copy-start.1 = (f32[4,16,128,128]{3,2,1,0:T(8,128)S(1)}, f32[4,16,128,128]{3,2,1,0:T(8,128)}, u32[]{:S(2)}) copy-start(f32[4,16,128,128]{3,2,1,0:T(8,128)} %param.5) | copy-start | bytes 12582916
  337.0 63.7 %collective-permute-start.45 = (f32[8,128,128]{2,1,0:T(8,128)S(1)}, f32[8,128,128]{2,1,0:T(8,128)S(1)}, u32[]{:S(2)}, u32[]{:S(2)}) collective-permute-start(f32[8,128,128]{2,1,0:T(8,128)S(1)} %get-tuple-element.69), channel_id=1, source_target_pairs={{0,0},{1,9},{2,2},{3,11},{4,4},{5,13},{6,6},{7,15},{8,1},{9,8},{10... | collective-permute-start | bytes 1572872 | tf_op jit(solution)/shard_map/ppermute | solution.py:249
  337.7 62.9 %collective-permute-start.41 = (f32[8,128,128]{2,1,0:T(8,128)S(1)}, f32[8,128,128]{2,1,0:T(8,128)S(1)}, u32[]{:S(2)}, u32[]{:S(2)}) collective-permute-start(f32[8,128,128]{2,1,0:T(8,128)S(1)} %get-tuple-element.62), channel_id=1, source_target_pairs={{0,7},{1,14},{2,5},{3,12},{4,3},{5,10},{6,1},{7,8},{8,6},{9,15},{1... | collective-permute-start | bytes 1572872 | tf_op jit(solution)/shard_map/ppermute | solution.py:249
  376.7 24.0 %collective-permute-start.46 = (f32[8,128,128]{2,1,0:T(8,128)S(1)}, f32[8,128,128]{2,1,0:T(8,128)S(1)}, u32[]{:S(2)}, u32[]{:S(2)}) collective-permute-start(f32[8,128,128]{2,1,0:T(8,128)S(1)} %get-tuple-element.70), channel_id=1, source_target_pairs={{0,1},{1,8},{2,3},{3,10},{4,5},{5,12},{6,7},{7,14},{8,0},{9,9},{10... | collective-permute-start | bytes 1572872 | tf_op jit(solution)/shard_map/ppermute | solution.py:249
  387.8 14.3 %collective-permute-start.47 = (f32[8,128,128]{2,1,0:T(8,128)S(1)}, f32[8,128,128]{2,1,0:T(8,128)S(1)}, u32[]{:S(2)}, u32[]{:S(2)}) collective-permute-start(f32[8,128,128]{2,1,0:T(8,128)S(1)} %get-tuple-element.71), channel_id=1, source_target_pairs={{0,2},{1,11},{2,0},{3,9},{4,6},{5,15},{6,4},{7,13},{8,3},{9,10},{1... | collective-permute-start | bytes 1572872 | tf_op jit(solution)/shard_map/ppermute | solution.py:249
  387.9 26.0 %collective-permute-start.48 = (f32[8,128,128]{2,1,0:T(8,128)S(1)}, f32[8,128,128]{2,1,0:T(8,128)S(1)}, u32[]{:S(2)}, u32[]{:S(2)}) collective-permute-start(f32[8,128,128]{2,1,0:T(8,128)S(1)} %get-tuple-element.72), channel_id=1, source_target_pairs={{0,3},{1,10},{2,1},{3,8},{4,7},{5,14},{6,5},{7,12},{8,2},{9,11},{1... | collective-permute-start | bytes 1572872 | tf_op jit(solution)/shard_map/ppermute | solution.py:249
  402.3 11.6 %copy-start.2 = (f32[4,16,128,128]{3,2,1,0:T(8,128)}, f32[4,16,128,128]{3,2,1,0:T(8,128)S(1)}, u32[]{:S(2)}) copy-start(f32[4,16,128,128]{3,2,1,0:T(8,128)S(1)} %fusion.1) | copy-start | bytes 12582916
